TPU v7x, 512 devices: a whole 4x4x16 slice. The times are simulated.
512 devices in a mesh: case: 8 (over z_hi, y), tile: 64 (over z_lo, x, core).
Axes of the slice: x: 4, y: 4, z: 16 (z_hi: 2, z_lo: 8; z = z_hi * 8 + z_lo), core: 2. Of those that a mesh axis runs over, the one named last changes fastest.
Arguments:
- density: float32 [512, 64, 256], P('tile', 'case'), may hold values from 0.05 to 1
- heat_power: float32 [8, 512, 64, 256], P('case', 'tile'), may hold values from 0.2 to 15, as said below
- laser_mask: int32 [8, 512, 64, 256], P('case', 'tile'), may hold values 0 or 1
- sink_mask: int32 [512, 64, 256], P('tile'), may hold values 0 or 1
Outputs:
- sensitivity: float32 [512, 64, 256], P('tile', 'case')
- objective: float32 [8], P('case')
Inputs may be any that keep to these rules, and one draw needn't show every extreme that they name: `heat_power`: positive heat power of each voxel and case.
All inputs are finite; a program needn't handle non-finite values. Where the computation divides by a largest or mean magnitude, that divisor is 1e-20 or more. No bound on the sum of `laser_mask` or of `sink_mask` on one device may be relied on, other than what follows from the above.
Results may differ from a plain program's by a relative error of at most 0.0001.
Values sent between devices are 32-bit elements; how exact they have to be, the bound alone decides.
A program may use at most 64 MiB of HBM per device.

v0:
```python
import jax
import jax.numpy as jnp
from jax import lax
from jax.sharding import PartitionSpec as P

SWEEPS = 6


heat_loss = 0.02
low_cond = 0.01
eig_low = 0.08
eig_high = 2.0


def with_halo(cells, sides, width):
    for axis, dim in sides:
        count = lax.axis_size(axis)
        ends = count - 1
        head = lax.slice_in_dim(cells, 0, width, axis=dim)
        tail = lax.slice_in_dim(cells, cells.shape[dim] - width, cells.shape[dim], axis=dim)
        cells = jnp.concatenate(
            [
                lax.ppermute(tail, axis, [(i, (i + 1) % count) for i in range(ends)]),
                cells,
                lax.ppermute(head, axis, [((i + 1) % count, i) for i in range(ends)]),
            ],
            axis=dim,
        )
    return cells


def pad_axis(field, along, leading, trailing):
    along = along % field.ndim
    widths = [(0, 0)] * field.ndim
    widths[along] = (leading, trailing)
    return jnp.pad(field, widths)


def lower_part(field, along):
    along = along % field.ndim
    return lax.slice_in_dim(field, 0, field.shape[along] - 1, axis=along)


def upper_part(field, along):
    along = along % field.ndim
    return lax.slice_in_dim(field, 1, field.shape[along], axis=along)


def flux_sum(field, face_cond, along):
    heat_flow = face_cond * (lower_part(field, along) - upper_part(field, along))
    return pad_axis(heat_flow, along, 0, 1) - pad_axis(heat_flow, along, 1, 0)


def interface_heatflow_pairs(left_field, right_field, along):
    multiplied_pieces = (lower_part(left_field, along) - upper_part(left_field, along)) * (
        lower_part(right_field, along) - upper_part(right_field, along)
    )
    return pad_axis(multiplied_pieces, along, 0, 1) + pad_axis(multiplied_pieces, along, 1, 0)


def beside_sum(field, along):
    return pad_axis(upper_part(field, along), along, 0, 1) + pad_axis(
        lower_part(field, along), along, 1, 0
    )


def edge_count(position, extent):
    return (position > 0).astype(jnp.float32) + (position < extent - 1).astype(jnp.float32)


def polynomial_relaxer(right_side, operate, diagonal_entries, unfixed_cells):
    centre = 0.5 * (eig_high + eig_low)
    half_width = 0.5 * (eig_high - eig_low)
    spread_ratio = centre / half_width
    weight_prev = 1.0 / spread_ratio
    iterate = unfixed_cells * right_side / diagonal_entries / centre
    update = iterate
    for sweep_idx in range(1, SWEEPS):
        weight_next = 1.0 / (2.0 * spread_ratio - weight_prev)
        residual_part = right_side - operate(iterate)
        update = weight_next * weight_prev * update + 2.0 * weight_next / half_width * (
            unfixed_cells * residual_part / diagonal_entries
        )
        iterate = iterate + update
        weight_prev = weight_next
    return iterate


def conduction(density_ext, ext_rows, grid_rows, column_count, depth_count):
    middle = density_ext[1:-1]
    beside_all = density_ext[:-2] + density_ext[2:] + beside_sum(middle, 1) + beside_sum(middle, 2)
    phys_rows = ext_rows[1:-1]
    rim_counts = 2.0 + edge_count(phys_rows, grid_rows)[:, None, None] + column_count + depth_count
    physical_rim = (2.0 * middle + beside_all) / rim_counts
    conduct_rim = low_cond + (1.0 - low_cond) * (physical_rim * physical_rim * physical_rim)
    inside = ((phys_rows >= 0) & (phys_rows < grid_rows)).astype(jnp.float32)
    face_ok = (inside[:-1] * inside[1:])[:, None, None]
    face_rows = 0.5 * (conduct_rim[:-1] + conduct_rim[1:]) * face_ok
    physical = physical_rim[1:-1]
    conduct = conduct_rim[1:-1]
    face_cols = 0.5 * (lower_part(conduct, 1) + upper_part(conduct, 1))
    face_deep = 0.5 * (lower_part(conduct, 2) + upper_part(conduct, 2))
    diagonal_entries = heat_loss + face_rows[:-1] + face_rows[1:]
    diagonal_entries = (
        diagonal_entries + pad_axis(face_cols, 1, 0, 1) + pad_axis(face_cols, 1, 1, 0)
    )
    diagonal_entries = (
        diagonal_entries + pad_axis(face_deep, 2, 0, 1) + pad_axis(face_deep, 2, 1, 0)
    )
    return (physical, face_rows, face_cols, face_deep, diagonal_entries, face_ok)


def body(density, heat_power, laser_mask, sink_mask):
    tile_rows, grid_y, grid_z = sink_mask.shape
    owned_y = density.shape[1]
    tile_count = lax.axis_size("tile")
    tile_at = lax.axis_index("tile")
    case_at = lax.axis_index("case")
    first_row = tile_at * tile_rows
    grid_rows = tile_rows * tile_count
    depth_count = edge_count(jnp.arange(grid_z), grid_z)[None, None, :]
    column_count = edge_count(jnp.arange(grid_y), grid_y)[None, :, None]
    full_rows = lax.all_gather(density, "case", axis=1, tiled=True)
    unfixed_cells = 1.0 - sink_mask.astype(jnp.float32)
    desired_values = laser_mask[0].astype(jnp.float32)
    source_term = desired_values * heat_power[0]
    density_rim = with_halo(full_rows, (("tile", 0),), 2)
    rim_source_rows = first_row - 2 + jnp.arange(tile_rows + 4)
    physical, face_rows, face_cols, face_deep, diagonal_entries, face_ok = conduction(
        density_rim, rim_source_rows, grid_rows, column_count, depth_count
    )

    def operate_rim(extended):
        own_cells = extended[..., 1:-1, :, :]
        heat_flow = face_rows * (extended[..., :-1, :, :] - extended[..., 1:, :, :])
        cross_rows = heat_flow[..., 1:, :, :] - heat_flow[..., :-1, :, :]
        return (
            heat_loss * own_cells
            + cross_rows
            + flux_sum(own_cells, face_cols, -2)
            + flux_sum(own_cells, face_deep, -1)
        )

    def primal_halo_strip(field):
        return with_halo(field, (("tile", 0),), 1)

    def rim_adjoint(field):
        return with_halo(field, (("tile", 0),), 1)

    def apply_forward_operator(field):
        return operate_rim(primal_halo_strip(field))

    def operate_adjoint(field):
        return operate_rim(rim_adjoint(field))

    thermal_state_grid = polynomial_relaxer(
        source_term, apply_forward_operator, diagonal_entries, unfixed_cells
    )
    thermal_halo_strip = primal_halo_strip(thermal_state_grid)
    dual_state_values = polynomial_relaxer(
        desired_values, operate_adjoint, diagonal_entries, unfixed_cells
    )
    adjoint_rim = rim_adjoint(dual_state_values)
    goal_derivative = jnp.sum(desired_values * thermal_state_grid)
    objective_total = lax.psum(goal_derivative, "tile")
    row_products = (
        (thermal_halo_strip[:-1] - thermal_halo_strip[1:])
        * (adjoint_rim[:-1] - adjoint_rim[1:])
        * face_ok
    )
    multiplied_pieces = (
        row_products[:-1]
        + row_products[1:]
        + interface_heatflow_pairs(thermal_state_grid, dual_state_values, 1)
        + interface_heatflow_pairs(thermal_state_grid, dual_state_values, 2)
    )
    sens_phys = -1.5 * (1.0 - low_cond) * (physical * physical) * multiplied_pieces
    own_rows = first_row + jnp.arange(tile_rows)
    row_count = edge_count(own_rows, grid_rows)[:, None, None]
    summed_all = lax.psum(sens_phys, "case")
    tile_counts = 2.0 + row_count + column_count + depth_count
    weighted = summed_all / tile_counts
    weighted_rim = with_halo(weighted, (("tile", 0),), 1)
    full_density = (
        2.0 * weighted
        + weighted_rim[:-2]
        + weighted_rim[2:]
        + beside_sum(weighted, 1)
        + beside_sum(weighted, 2)
    )
    sens_density = lax.dynamic_slice_in_dim(full_density, case_at * owned_y, owned_y, 1)
    local_abs = jnp.sum(jnp.abs(sens_density))
    all_cells = grid_rows * grid_y * grid_z
    abs_total = lax.psum(local_abs, ("case", "tile"))
    magnitude = abs_total / all_cells
    return (sens_density / (magnitude + 1e-06), objective_total.reshape(1))


def solution(mesh):
    return jax.shard_map(
        body,
        mesh=mesh,
        in_specs=(
            P("tile", "case", None),
            P("case", "tile", None, None),
            P("case", "tile", None, None),
            P("tile", None, None),
        ),
        out_specs=(P("tile", "case", None), P("case")),
        check_vma=False,
    )
```

profile of v0, /device:TPU:1, one launch (start us, length us, event | category | flops | bytes accessed | tf_op | source)
XLA Modules:
  0.0 537.1 jit_solution(6902468820926930077)
XLA Ops:
  7.2 64.9 %all_gather.3 = f32[8,64,256]{2,1,0:T(8,128)S(1)} all-gather(f32[8,8,256]{2,1,0:T(8,128)} %param.4), channel_id=1, replica_groups=mesh['case'=8,'tile'=64] {'case'}, dimensions={1}, use_global_device_ids=true | all-gather | bytes 589824 | tf_op jit(solution)/shard_map/all_gather | solution.py:123
  72.2 7.7 %collective-permute-start = (f32[2,64,256]{2,1,0:T(8,128)S(1)}, f32[2,64,256]{2,1,0:T(8,128)S(1)}, u32[]{:S(2)}, u32[]{:S(2)}) collective-permute-start(f32[2,64,256]{2,1,0:T(8,128)S(1)} %get-tuple-element.66), channel_id=1, source_target_pairs={{0,1},{1,2},{2,3},{3,4},{4,5},{5,6},{6,7},{7,8},{8,9},{9,10},{10,1... | collective-permute-start | bytes 393224 | tf_op jit(solution)/shard_map/ppermute | solution.py:23
  82.2 4.0 collective-permute-done.1
  91.0 2.4 collective-permute-start.15
  93.8 2.8 collective-permute-done.15
  99.4 2.4 collective-permute-start.17
  102.2 2.8 collective-permute-done.17
  107.8 2.4 collective-permute-start.19
  110.6 5.3 collective-permute-done.19
  116.8 1.9 collective-permute-start.20
  118.7 2.4 collective-permute-start.21
  121.5 4.9 collective-permute-done.21
  129.3 2.4 collective-permute-start.23
  132.1 4.9 collective-permute-done.23
  140.3 2.4 collective-permute-start.3
  142.8 5.3 collective-permute-start.24
  150.8 3.6 collective-permute-start.4
  154.5 2.1 collective-permute-start.5
  156.9 3.5 collective-permute-done.5
  161.3 2.4 collective-permute-start.6
  166.1 4.9 collective-permute-done.7
  173.8 2.4 collective-permute-start.9
  176.6 4.9 collective-permute-done.9
  182.4 2.1 collective-permute-start.10
  184.5 2.2 collective-permute-start.11
  187.1 9.0 %collective-permute-done.11 = f32[1,64,256]{2,1,0:T(8,128)S(1)} collective-permute-done((f32[1,64,256]{2,1,0:T(8,128)S(1)}, f32[1,64,256]{2,1,0:T(8,128)S(1)}, u32[]{:S(2)}, u32[]{:S(2)}) %collective-permute-start.11) | collective-permute-done | bytes 65568 | tf_op jit(solution)/shard_map/ppermute | solution.py:25
  197.7 1.9 collective-permute-start.12
  199.6 2.4 collective-permute-start.13
  202.4 4.6 collective-permute-done.13
  208.4 208.7 %psum.23 = f32[1]{0:T(128)} all-reduce(f32[1]{0:T(128)} %bitcast.2), channel_id=1, replica_groups=mesh['case'=8,'tile'=64] {'tile'}, use_global_device_ids=true, to_apply=%region_4.5 | all-reduce | flops 1 | bytes 8 | tf_op jit(solution)/shard_map/psum | solution.py:165
  420.3 6.1 %collective-permute-start.27 = (f32[1,64,256]{2,1,0:T(8,128)S(1)}, f32[1,64,256]{2,1,0:T(8,128)S(1)}, u32[]{:S(2)}, u32[]{:S(2)}) collective-permute-start(f32[1,64,256]{2,1,0:T(8,128)S(1)} %get-tuple-element.36), channel_id=1, source_target_pairs={{1,0},{2,1},{3,2},{4,3},{5,4},{6,5},{7,6},{8,7},{9,8},{10,9},{11,1... | collective-permute-start | bytes 196616 | tf_op jit(solution)/shard_map/ppermute | solution.py:25
  428.0 100.9 %psum.22 = f32[]{:T(128)} all-reduce(f32[]{:T(128)} %get-tuple-element.4), channel_id=1, replica_groups=mesh['case'=8,'tile'=64] {'case','tile'}, use_global_device_ids=true, to_apply=%region_2.3 | all-reduce | flops 1 | bytes 8 | tf_op jit(solution)/shard_map/psum | solution.py:194
  (118 shorter events, 40.7 us)
Async XLA Ops:
  7.2 409.9 %all-reduce.58.cloned.1.call-start = ((), (), s32[]{:S(2)}) async-start(), calls=%async_computation | async-start | bytes 1048576 | tf_op jit(solution)/shard_map/psum | solution.py:180
  72.2 10.0 %collective-permute-start = (f32[2,64,256]{2,1,0:T(8,128)S(1)}, f32[2,64,256]{2,1,0:T(8,128)S(1)}, u32[]{:S(2)}, u32[]{:S(2)}) collective-permute-start(f32[2,64,256]{2,1,0:T(8,128)S(1)} %get-tuple-element.66), channel_id=1, source_target_pairs={{0,1},{1,2},{2,3},{3,4},{4,5},{5,6},{6,7},{7,8},{8,9},{9,10},{10,1... | collective-permute-start | bytes 393224 | tf_op jit(solution)/shard_map/ppermute | solution.py:23
  79.9 6.3 %collective-permute-start.1 = (f32[2,64,256]{2,1,0:T(8,128)S(1)}, f32[2,64,256]{2,1,0:T(8,128)S(1)}, u32[]{:S(2)}, u32[]{:S(2)}) collective-permute-start(f32[2,64,256]{2,1,0:T(8,128)S(1)} %get-tuple-element.65), channel_id=1, source_target_pairs={{1,0},{2,1},{3,2},{4,3},{5,4},{6,5},{7,6},{8,7},{9,8},{10,9},{11,1... | collective-permute-start | bytes 393224 | tf_op jit(solution)/shard_map/ppermute | solution.py:25
  87.4 1.0 copy-start
  87.4 1.2 copy-start.1
  89.1 4.7 collective-permute-start.14
  91.0 5.6 %collective-permute-start.15 = (f32[1,64,256]{2,1,0:T(8,128)S(1)}, f32[1,64,256]{2,1,0:T(8,128)S(1)}, u32[]{:S(2)}, u32[]{:S(2)}) collective-permute-start(f32[1,64,256]{2,1,0:T(8,128)S(1)} %get-tuple-element.51), channel_id=1, source_target_pairs={{1,0},{2,1},{3,2},{4,3},{5,4},{6,5},{7,6},{8,7},{9,8},{10,9},{11,1... | collective-permute-start | bytes 196616 | tf_op jit(solution)/shard_map/ppermute | solution.py:25
  97.5 4.7 collective-permute-start.16
  99.4 5.6 %collective-permute-start.17 = (f32[1,64,256]{2,1,0:T(8,128)S(1)}, f32[1,64,256]{2,1,0:T(8,128)S(1)}, u32[]{:S(2)}, u32[]{:S(2)}) collective-permute-start(f32[1,64,256]{2,1,0:T(8,128)S(1)} %get-tuple-element.49), channel_id=1, source_target_pairs={{1,0},{2,1},{3,2},{4,3},{5,4},{6,5},{7,6},{8,7},{9,8},{10,9},{11,1... | collective-permute-start | bytes 196616 | tf_op jit(solution)/shard_map/ppermute | solution.py:25
  105.9 4.7 collective-permute-start.18
  107.8 8.0 %collective-permute-start.19 = (f32[1,64,256]{2,1,0:T(8,128)S(1)}, f32[1,64,256]{2,1,0:T(8,128)S(1)}, u32[]{:S(2)}, u32[]{:S(2)}) collective-permute-start(f32[1,64,256]{2,1,0:T(8,128)S(1)} %get-tuple-element.47), channel_id=1, source_target_pairs={{1,0},{2,1},{3,2},{4,3},{5,4},{6,5},{7,6},{8,7},{9,8},{10,9},{11,1... | collective-permute-start | bytes 196616 | tf_op jit(solution)/shard_map/ppermute | solution.py:25
  116.8 4.7 collective-permute-start.20
  118.7 7.7 %collective-permute-start.21 = (f32[1,64,256]{2,1,0:T(8,128)S(1)}, f32[1,64,256]{2,1,0:T(8,128)S(1)}, u32[]{:S(2)}, u32[]{:S(2)}) collective-permute-start(f32[1,64,256]{2,1,0:T(8,128)S(1)} %get-tuple-element.45), channel_id=1, source_target_pairs={{1,0},{2,1},{3,2},{4,3},{5,4},{6,5},{7,6},{8,7},{9,8},{10,9},{11,1... | collective-permute-start | bytes 196616 | tf_op jit(solution)/shard_map/ppermute | solution.py:25
  127.4 4.7 collective-permute-start.22
  129.3 7.7 %collective-permute-start.23 = (f32[1,64,256]{2,1,0:T(8,128)S(1)}, f32[1,64,256]{2,1,0:T(8,128)S(1)}, u32[]{:S(2)}, u32[]{:S(2)}) collective-permute-start(f32[1,64,256]{2,1,0:T(8,128)S(1)} %get-tuple-element.43), channel_id=1, source_target_pairs={{1,0},{2,1},{3,2},{4,3},{5,4},{6,5},{7,6},{8,7},{9,8},{10,9},{11,1... | collective-permute-start | bytes 196616 | tf_op jit(solution)/shard_map/ppermute | solution.py:25
  132.0 5.1 copy-start.2
  138.4 11.6 %collective-permute-start.2 = (f32[1,64,256]{2,1,0:T(8,128)S(1)}, f32[1,64,256]{2,1,0:T(8,128)S(1)}, u32[]{:S(2)}, u32[]{:S(2)}) collective-permute-start(f32[1,64,256]{2,1,0:T(8,128)S(1)} %get-tuple-element.64), channel_id=1, source_target_pairs={{0,1},{1,2},{2,3},{3,4},{4,5},{5,6},{6,7},{7,8},{8,9},{9,10},{10,1... | collective-permute-start | bytes 196616 | tf_op jit(solution)/shard_map/ppermute | solution.py:23
  140.3 9.6 %collective-permute-start.3 = (f32[1,64,256]{2,1,0:T(8,128)S(1)}, f32[1,64,256]{2,1,0:T(8,128)S(1)}, u32[]{:S(2)}, u32[]{:S(2)}) collective-permute-start(f32[1,64,256]{2,1,0:T(8,128)S(1)} %get-tuple-element.63), channel_id=1, source_target_pairs={{1,0},{2,1},{3,2},{4,3},{5,4},{6,5},{7,6},{8,7},{9,8},{10,9},{11,1... | collective-permute-start | bytes 196616 | tf_op jit(solution)/shard_map/ppermute | solution.py:25
  142.8 59.6 %collective-permute-start.24 = (f32[1,64,256]{2,1,0:T(8,128)S(1)}, f32[1,64,256]{2,1,0:T(8,128)S(1)}, u32[]{:S(2)}, u32[]{:S(2)}) collective-permute-start(f32[1,64,256]{2,1,0:T(8,128)S(1)} %get-tuple-element.42), channel_id=1, source_target_pairs={{0,1},{1,2},{2,3},{3,4},{4,5},{5,6},{6,7},{7,8},{8,9},{9,10},{10,1... | collective-permute-start | bytes 196616 | tf_op jit(solution)/shard_map/ppermute | solution.py:23
  148.0 54.3 %collective-permute-start.25 = (f32[1,64,256]{2,1,0:T(8,128)S(1)}, f32[1,64,256]{2,1,0:T(8,128)S(1)}, u32[]{:S(2)}, u32[]{:S(2)}) collective-permute-start(f32[1,64,256]{2,1,0:T(8,128)S(1)} %get-tuple-element.41), channel_id=1, source_target_pairs={{1,0},{2,1},{3,2},{4,3},{5,4},{6,5},{7,6},{8,7},{9,8},{10,9},{11,1... | collective-permute-start | bytes 196616 | tf_op jit(solution)/shard_map/ppermute | solution.py:25
  150.8 6.1 %collective-permute-start.4 = (f32[1,64,256]{2,1,0:T(8,128)S(1)}, f32[1,64,256]{2,1,0:T(8,128)S(1)}, u32[]{:S(2)}, u32[]{:S(2)}) collective-permute-start(f32[1,64,256]{2,1,0:T(8,128)S(1)} %get-tuple-element.62), channel_id=1, source_target_pairs={{0,1},{1,2},{2,3},{3,4},{4,5},{5,6},{6,7},{7,8},{8,9},{9,10},{10,1... | collective-permute-start | bytes 196616 | tf_op jit(solution)/shard_map/ppermute | solution.py:23
  154.5 6.0 %collective-permute-start.5 = (f32[1,64,256]{2,1,0:T(8,128)S(1)}, f32[1,64,256]{2,1,0:T(8,128)S(1)}, u32[]{:S(2)}, u32[]{:S(2)}) collective-permute-start(f32[1,64,256]{2,1,0:T(8,128)S(1)} %get-tuple-element.61), channel_id=1, source_target_pairs={{1,0},{2,1},{3,2},{4,3},{5,4},{6,5},{7,6},{8,7},{9,8},{10,9},{11,1... | collective-permute-start | bytes 196616 | tf_op jit(solution)/shard_map/ppermute | solution.py:25
  161.3 4.7 collective-permute-start.6
  163.8 7.2 %collective-permute-start.7 = (f32[1,64,256]{2,1,0:T(8,128)S(1)}, f32[1,64,256]{2,1,0:T(8,128)S(1)}, u32[]{:S(2)}, u32[]{:S(2)}) collective-permute-start(f32[1,64,256]{2,1,0:T(8,128)S(1)} %get-tuple-element.59), channel_id=1, source_target_pairs={{1,0},{2,1},{3,2},{4,3},{5,4},{6,5},{7,6},{8,7},{9,8},{10,9},{11,1... | collective-permute-start | bytes 196616 | tf_op jit(solution)/shard_map/ppermute | solution.py:25
  171.9 4.7 collective-permute-start.8
  173.8 7.7 %collective-permute-start.9 = (f32[1,64,256]{2,1,0:T(8,128)S(1)}, f32[1,64,256]{2,1,0:T(8,128)S(1)}, u32[]{:S(2)}, u32[]{:S(2)}) collective-permute-start(f32[1,64,256]{2,1,0:T(8,128)S(1)} %get-tuple-element.57), channel_id=1, source_target_pairs={{1,0},{2,1},{3,2},{4,3},{5,4},{6,5},{7,6},{8,7},{9,8},{10,9},{11,1... | collective-permute-start | bytes 196616 | tf_op jit(solution)/shard_map/ppermute | solution.py:25
  182.4 4.7 collective-permute-start.10
  184.5 11.6 %collective-permute-start.11 = (f32[1,64,256]{2,1,0:T(8,128)S(1)}, f32[1,64,256]{2,1,0:T(8,128)S(1)}, u32[]{:S(2)}, u32[]{:S(2)}) collective-permute-start(f32[1,64,256]{2,1,0:T(8,128)S(1)} %get-tuple-element.55), channel_id=1, source_target_pairs={{1,0},{2,1},{3,2},{4,3},{5,4},{6,5},{7,6},{8,7},{9,8},{10,9},{11,1... | collective-permute-start | bytes 196616 | tf_op jit(solution)/shard_map/ppermute | solution.py:25
  197.7 4.7 collective-permute-start.12
  199.6 7.4 %collective-permute-start.13 = (f32[1,64,256]{2,1,0:T(8,128)S(1)}, f32[1,64,256]{2,1,0:T(8,128)S(1)}, u32[]{:S(2)}, u32[]{:S(2)}) collective-permute-start(f32[1,64,256]{2,1,0:T(8,128)S(1)} %get-tuple-element.53), channel_id=1, source_target_pairs={{1,0},{2,1},{3,2},{4,3},{5,4},{6,5},{7,6},{8,7},{9,8},{10,9},{11,1... | collective-permute-start | bytes 196616 | tf_op jit(solution)/shard_map/ppermute | solution.py:25
  418.4 8.3 %collective-permute-start.26 = (f32[1,64,256]{2,1,0:T(8,128)S(1)}, f32[1,64,256]{2,1,0:T(8,128)S(1)}, u32[]{:S(2)}, u32[]{:S(2)}) collective-permute-start(f32[1,64,256]{2,1,0:T(8,128)S(1)} %get-tuple-element.35), channel_id=1, source_target_pairs={{0,1},{1,2},{2,3},{3,4},{4,5},{5,6},{6,7},{7,8},{8,9},{9,10},{10,1... | collective-permute-start | bytes 196616 | tf_op jit(solution)/shard_map/ppermute | solution.py:23
  420.3 7.0 %collective-permute-start.27 = (f32[1,64,256]{2,1,0:T(8,128)S(1)}, f32[1,64,256]{2,1,0:T(8,128)S(1)}, u32[]{:S(2)}, u32[]{:S(2)}) collective-permute-start(f32[1,64,256]{2,1,0:T(8,128)S(1)} %get-tuple-element.36), channel_id=1, source_target_pairs={{1,0},{2,1},{3,2},{4,3},{5,4},{6,5},{7,6},{8,7},{9,8},{10,9},{11,1... | collective-permute-start | bytes 196616 | tf_op jit(solution)/shard_map/ppermute | solution.py:25
Sparse Core Ops, SparseCore 0:
  208.4 170.4 all-reduce.57
where the time goes:
time: 538 us; the launch traced here: 537 us
  blocking collectives  375 us (70%)
  starting transfers between devices  74 us (14%)
  waiting for transfers between devices  52.4 us (10%)
  other arithmetic  18.8 us (3%)
  between operations  15.5 us (3%)
    psum x1, blocking collectives, body(): objective_total = lax.psum(goal_derivative, 'tile')  209 us
    psum x1, blocking collectives, body(): abs_total = lax.psum(local_abs, ('case', 'tile'))  101 us
    all_gather x1, blocking collectives, body(): full_rows = lax.all_gather(density, 'case', axis=1, tiled=True)  64.9 us
    ppermute x14, waiting for transfers between devices, with_halo(): lax.ppermute(head, axis, [((i + 1) % count, i) for i in range(ends)])  52.3 us
    ppermute x14, starting transfers between devices, with_halo(): lax.ppermute(tail, axis, [(i, (i + 1) % count) for i in range(ends)])  38.5 us
    ppermute x14, starting transfers between devices, with_halo(): lax.ppermute(head, axis, [((i + 1) % count, i) for i in range(ends)])  35.4 us
  transfers between devices with their start and end apart: 29, of which 12 were waited for; matrix products, arithmetic and copies ran while one was open for 2% of the time, Pallas kernels for 0%

commit v1 on v0

v1 whole, which is shorter than its diff:
```python
import functools

import jax
import jax.numpy as jnp
from jax import lax
from jax.experimental import pallas as pl
from jax.experimental.pallas import tpu as pltpu
from jax.sharding import PartitionSpec as P

SWEEPS = 6
heat_loss = 0.02
low_cond = 0.01
eig_low = 0.08
eig_high = 2.0

MESH = pl.DeviceIdType.MESH
YD = 4
ZH = 2
XC = 8
R = 8
EXT = 3 * R


def horner_coefficients():
    centre = 0.5 * (eig_high + eig_low)
    half = 0.5 * (eig_high - eig_low)
    ratio = centre / half
    weight = 1.0 / ratio
    x = [1.0 / centre] + [0.0] * (SWEEPS - 1)
    s = list(x)
    for _ in range(1, SWEEPS):
        nxt = 1.0 / (2.0 * ratio - weight)
        r = [-a for a in x]
        r[0] += 1.0
        for k in range(1, SWEEPS):
            r[k] += x[k - 1]
        s = [nxt * weight * a + 2.0 * nxt / half * b for a, b in zip(s, r)]
        x = [a + b for a, b in zip(x, s)]
        weight = nxt
    return x


COEF = horner_coefficients()
LEAD = COEF[-1]


def kernel(
    tiles,
    dens_in, heat_in, laser_in, sink_in,
    sens_out, obj_out,
    dens, heat, laser, sink, src, cond, wgt, kxm, kxp, kym, kyp, kzm, kzp, bias, ya, yb,
    part, rfar, rnear, fsum, rz, qsum, qhalo, sens, msg, arx, ary, arz,
    lsem, s_y, r_y, s_z, r_z, s_yf, r_yf, s_t, r_t, s_h, r_h, s_p, r_p, s_pz, r_pz, s_q, r_q,
    s_ax, r_ax, s_ay, r_ay, s_az, r_az,
):
    zl_n = tiles // XC
    z_n = ZH * zl_n
    c = lax.axis_index("case")
    t = lax.axis_index("tile")
    zh = c // YD
    yy = c % YD
    zl = t // XC
    xc = t % XC
    z = zh * zl_n + zl
    has_left = t > 0
    has_right = t < tiles - 1
    halves = dens.shape[1]
    width = 128 * halves

    def y_case(d):
        return zh * YD + (yy + d) % YD

    def z_dev(d):
        zz = (z + d) % z_n
        return {"case": (zz // zl_n) * YD + yy, "tile": (zz % zl_n) * XC + xc}

    def x_tile(d):
        return zl * XC + (xc + d) % XC

    barrier = pltpu.get_barrier_semaphore()

    def greet(dev):
        pl.semaphore_signal(barrier, inc=1, device_id=dev, device_id_type=MESH)

    for d in range(1, z_n):
        greet(z_dev(d))
    for d in range(1, YD):
        greet({"case": y_case(d), "tile": t})
    for d in range(1, XC):
        greet({"case": c, "tile": x_tile(d)})

    @pl.when(has_left)
    def _():
        greet({"case": c, "tile": t - 1})

    @pl.when(has_right)
    def _():
        greet({"case": c, "tile": t + 1})

    slab = pl.ds(pl.multiple_of(c * R, R), R)
    loads = []
    for h in range(halves):
        lanes = pl.ds(h * 128, 128)
        loads.append([
            pltpu.make_async_copy(dens_in.at[:, :, lanes], dens.at[pl.ds(R, R), h, slab, :], lsem.at[h, 0]),
            pltpu.make_async_copy(heat_in.at[0, :, :, lanes], heat.at[:, h], lsem.at[h, 1]),
            pltpu.make_async_copy(laser_in.at[0, :, :, lanes], laser.at[:, h], lsem.at[h, 2]),
            pltpu.make_async_copy(sink_in.at[:, :, lanes], sink.at[pl.ds(R, R), h], lsem.at[h, 3]),
        ])
    for k in range(4):
        for h in range(halves):
            loads[h][k].start()

    @pl.when(t == 0)
    def _():
        dens[0:R] = jnp.zeros((R,) + dens.shape[1:], jnp.float32)
        src[2:R] = jnp.zeros((R - 2,) + src.shape[1:], jnp.float32)
        sink[2:R] = jnp.zeros((R - 2,) + sink.shape[1:], jnp.int32)
        qhalo[0] = jnp.zeros(qhalo.shape[1:], jnp.float32)

    @pl.when(t == tiles - 1)
    def _():
        dens[2 * R:] = jnp.zeros((R,) + dens.shape[1:], jnp.float32)
        src[2 * R:3 * R - 2] = jnp.zeros((R - 2,) + src.shape[1:], jnp.float32)
        sink[2 * R:3 * R - 2] = jnp.zeros((R - 2,) + sink.shape[1:], jnp.int32)
        qhalo[1] = jnp.zeros(qhalo.shape[1:], jnp.float32)

    for k in range(3):
        for h in range(halves):
            loads[h][k].wait()

    def row_load(ref, l, j):
        return jnp.concatenate([ref[l, h, pl.ds(j, R, stride=R), :] for h in range(halves)], axis=1)

    def make_source(l, carry):
        for j in range(R):
            src[l + R, j] = row_load(heat, l, j) * row_load(laser, l, j).astype(jnp.float32)
        return carry

    lax.fori_loop(0, R, make_source, 0)

    for h in range(halves):
        loads[h][3].wait()
    pl.semaphore_wait(
        barrier, (z_n - 1) + (YD - 1) + (XC - 1) + has_left.astype(jnp.int32) + has_right.astype(jnp.int32)
    )

    def remote(a, b, ssem, rsem, dev):
        return pltpu.make_async_remote_copy(
            src_ref=a, dst_ref=b, send_sem=ssem, recv_sem=rsem, device_id=dev, device_id_type=MESH
        )

    def to_left(a, b, ssem, rsem):
        return remote(a, b, ssem, rsem, {"case": c, "tile": jnp.maximum(t - 1, 0)})

    def to_right(a, b, ssem, rsem):
        return remote(a, b, ssem, rsem, {"case": c, "tile": jnp.minimum(t + 1, tiles - 1)})

    own = dens.at[pl.ds(R, R), :, slab, :]
    z_copy = remote(own, own, s_z.at[0], r_z.at[0], z_dev(zl_n))
    z_copy.start()
    y_copies = []
    for d in range(1, YD):
        cp = remote(own, own, s_y.at[d - 1], r_y.at[d - 1], {"case": y_case(d), "tile": t})
        cp.start()
        y_copies.append(cp)

    halo_left = [
        to_left(src.at[pl.ds(R, R - 2)], src.at[pl.ds(2 * R, R - 2)], s_h.at[0], r_h.at[1]),
        to_left(sink.at[pl.ds(R, R - 2)], sink.at[pl.ds(2 * R, R - 2)], s_h.at[1], r_h.at[3]),
    ]
    halo_right = [
        to_right(src.at[pl.ds(R + 2, R - 2)], src.at[pl.ds(2, R - 2)], s_h.at[2], r_h.at[0]),
        to_right(sink.at[pl.ds(R + 2, R - 2)], sink.at[pl.ds(2, R - 2)], s_h.at[3], r_h.at[2]),
    ]

    def send_sides(left, right):
        @pl.when(has_left)
        def _():
            for cp in left:
                cp.start()

        @pl.when(has_right)
        def _():
            for cp in right:
                cp.start()

    send_sides(halo_left, halo_right)

    def slab_of(case):
        return pl.ds(pl.multiple_of(case * R, R), R)

    tile_copies = []

    def forward(case, order):
        here = dens.at[pl.ds(R, R), :, slab_of(case), :]
        left = to_left(here, dens.at[pl.ds(2 * R, R), :, slab_of(case), :], s_t.at[0, order], r_t.at[1, order])
        right = to_right(here, dens.at[pl.ds(0, R), :, slab_of(case), :], s_t.at[1, order], r_t.at[0, order])
        send_sides([left], [right])
        tile_copies.append((left, right))

    forward(c, 0)
    for d in range(1, YD):
        y_copies[d - 1].wait_recv()
        forward(zh * YD + (yy + YD - d) % YD, d)

    z_copy.wait_recv()
    far = (1 - zh) * YD
    far_case = far + yy
    far_ref = dens.at[pl.ds(R, R), :, slab_of(far_case), :]
    yf_copies = []
    for d in range(1, YD):
        cp = remote(far_ref, far_ref, s_yf.at[d - 1], r_yf.at[d - 1], {"case": y_case(d), "tile": t})
        cp.start()
        yf_copies.append(cp)
    forward(far_case, YD)
    for d in range(1, YD):
        yf_copies[d - 1].wait_recv()
        forward(far + (yy + YD - d) % YD, YD + d)

    @pl.when(has_left)
    def _():
        for left, right in tile_copies:
            right.wait_recv()
        for cp in halo_right:
            cp.wait_recv()

    @pl.when(has_right)
    def _():
        for left, right in tile_copies:
            left.wait_recv()
        for cp in halo_left:
            cp.wait_recv()

    lane = lax.broadcasted_iota(jnp.int32, (R, width), 1)
    sub = lax.broadcasted_iota(jnp.int32, (R, width), 0)
    z_first = lane == 0
    z_last = lane == width - 1
    y_first = sub == 0
    y_last = sub == R - 1
    zero = jnp.zeros((R, width), jnp.float32)
    one = jnp.ones((R, width), jnp.float32)
    grid_rows = tiles * R

    def z_prev(v):
        return pltpu.roll(v, 1, 1)

    def z_next(v):
        return pltpu.roll(v, width - 1, 1)

    def around(planes, j):
        before = planes[j - 1] if j > 0 else pltpu.roll(planes[R - 1], 1, 0)
        after = planes[j + 1] if j < R - 1 else pltpu.roll(planes[0], R - 1, 0)
        return before, after

    def flag(cond_):
        return cond_.astype(jnp.float32)

    def physical_step(e, carry):
        g = t * R - R + e
        nx = 2.0 + flag(g > 0) + flag(g < grid_rows - 1)
        nyz = nx + jnp.where(z_first | z_last, 1.0, 2.0)
        planes = [row_load(dens, e, j) for j in range(R)]
        for j in range(R):
            v = planes[j]
            before, after = around(planes, j)
            ny = jnp.full((R, width), 2.0)
            if j == 0:
                before = jnp.where(y_first, 0.0, before)
                ny = jnp.where(y_first, 1.0, 2.0)
            if j == R - 1:
                after = jnp.where(y_last, 0.0, after)
                ny = jnp.where(y_last, 1.0, 2.0)
            total = (
                2.0 * v + row_load(dens, e - 1, j) + row_load(dens, e + 1, j)
                + before + after
                + jnp.where(z_first, 0.0, z_prev(v)) + jnp.where(z_last, 0.0, z_next(v))
            )
            inv = 1.0 / (nyz + ny)
            phys = total * inv
            sq = phys * phys
            cond[e, j] = low_cond + (1.0 - low_cond) * (sq * phys)
            wgt[e, j] = (-1.5 * (1.0 - low_cond) * LEAD * LEAD) * sq * inv
        return carry

    lax.fori_loop(1, EXT - 1, physical_step, 0)

    def inside(g):
        return (g >= 0) & (g < grid_rows)

    def face_step(e, carry):
        g = t * R - R + e
        vm = 0.5 * flag(inside(g - 1) & inside(g))
        vp = 0.5 * flag(inside(g) & inside(g + 1))
        planes = [cond[e, j] for j in range(R)]
        for j in range(R):
            v = planes[j]
            before, after = around(planes, j)
            f_xm = vm * (cond[e - 1, j] + v)
            f_xp = vp * (cond[e + 1, j] + v)
            f_ym = 0.5 * (before + v)
            f_yp = 0.5 * (after + v)
            if j == 0:
                f_ym = jnp.where(y_first, 0.0, f_ym)
            if j == R - 1:
                f_yp = jnp.where(y_last, 0.0, f_yp)
            f_zm = jnp.where(z_first, 0.0, 0.5 * (z_prev(v) + v))
            f_zp = jnp.where(z_last, 0.0, 0.5 * (z_next(v) + v))
            diag = heat_loss + f_xm + f_xp + f_ym + f_yp + f_zm + f_zp
            free = jnp.where(row_load(sink, e, j) == 0, 1.0, 0.0)
            scale = free / diag
            kxm[e, j] = scale * f_xm
            kxp[e, j] = scale * f_xp
            kym[e, j] = scale * f_ym
            kyp[e, j] = scale * f_yp
            kzm[e, j] = scale * f_zm
            kzp[e, j] = scale * f_zp
            source = src[e, j]
            bias[0, e, j] = scale * source
            bias[1, e, j] = jnp.where(source > 0.0, scale, 0.0)
        return carry

    lax.fori_loop(2, EXT - 2, face_step, 0)

    def sweep(n, y_in, y_out):
        ratio = COEF[SWEEPS - 2 - n] / LEAD

        def step(e, carry):
            for j in range(R):
                ks = [k[e, j] for k in (kxm, kxp, kym, kyp, kzm, kzp)]
                for f in range(2):
                    v = y_in[f, e, j]
                    before = y_in[f, e, j - 1] if j > 0 else pltpu.roll(y_in[f, e, R - 1], 1, 0)
                    after = y_in[f, e, j + 1] if j < R - 1 else pltpu.roll(y_in[f, e, 0], R - 1, 0)
                    acc = ratio * bias[f, e, j]
                    acc = acc + ks[0] * y_in[f, e - 1, j]
                    acc = acc + ks[1] * y_in[f, e + 1, j]
                    acc = acc + ks[2] * before
                    acc = acc + ks[3] * after
                    acc = acc + ks[4] * z_prev(v)
                    acc = acc + ks[5] * z_next(v)
                    y_out[f, e, j] = acc
            return carry

        lax.fori_loop(3 + n, EXT - 3 - n, step, 0)

    bufs = [bias, ya, yb, ya, yb, ya]
    for n in range(SWEEPS - 1):
        sweep(n, bufs[n], bufs[n + 1])
    fin = bufs[SWEEPS - 1]

    def slab_store(row, value):
        for h in range(halves):
            part[h, pl.ds(row, R, stride=10 * R), :] = value[:, h * 128:(h + 1) * 128]

    def product_step(e, total):
        g = t * R - R + e
        l = e - R
        vm = flag(inside(g - 1))
        vp = flag(inside(g + 1))
        ps = [fin[0, e, j] for j in range(R)]
        qs = [fin[1, e, j] for j in range(R)]
        y_faces = []
        for j in range(R):
            pn = around(ps, j)[1]
            qn = around(qs, j)[1]
            face = (ps[j] - pn) * (qs[j] - qn)
            if j == R - 1:
                face = jnp.where(y_last, 0.0, face)
            y_faces.append(face)
        for j in range(R):
            p, q = ps[j], qs[j]
            acc = vm * ((p - fin[0, e - 1, j]) * (q - fin[1, e - 1, j]))
            acc = acc + vp * ((p - fin[0, e + 1, j]) * (q - fin[1, e + 1, j]))
            acc = acc + y_faces[j] + around(y_faces, j)[0]
            face = jnp.where(z_last, 0.0, (p - z_next(p)) * (q - z_next(q)))
            acc = (acc + face + z_prev(face)) * wgt[e, j]
            slab_store(l * R + j, acc)
            if j == R - 1:
                edge = jnp.where(y_first, 0.0, pltpu.roll(acc, 1, 0))
                slab_store(8 * R + l, edge)
            if j == 0:
                edge = jnp.where(y_last, 0.0, pltpu.roll(acc, R - 1, 0))
                slab_store(9 * R + l, edge)
            total = total + jnp.where(src[e, j] > 0.0, p, 0.0)
        return total

    obj_vec = lax.fori_loop(R, 2 * R, product_step, zero)

    def block(case):
        return pl.ds(pl.multiple_of(case * (10 * R), 10 * R), 10 * R)

    far_parts = []
    near_parts = []
    for d in range(1, YD):
        dest = (yy + d) % YD
        cp = remote(part.at[:, block(far + dest)], rfar.at[d - 1], s_p.at[0, d - 1], r_p.at[0, d - 1],
                    {"case": y_case(d), "tile": t})
        cp.start()
        far_parts.append(cp)
    for d in range(1, YD):
        dest = (yy + d) % YD
        cp = remote(part.at[:, block(zh * YD + dest)], rnear.at[d - 1], s_p.at[1, d - 1], r_p.at[1, d - 1],
                    {"case": y_case(d), "tile": t})
        cp.start()
        near_parts.append(cp)
    obj_part = LEAD * jnp.sum(obj_vec)
    for cp in far_parts:
        cp.wait_recv()
    base_far = far_case * (10 * R)

    def far_step(i, carry):
        rows = pl.ds(pl.multiple_of(i * R, R), R)
        mine = part[:, pl.ds(pl.multiple_of(base_far + i * R, R), R), :]
        fsum[:, rows, :] = (mine + rfar[0, :, rows, :]) + (rfar[1, :, rows, :] + rfar[2, :, rows, :])
        return carry

    lax.fori_loop(0, 10, far_step, 0)
    pz = remote(fsum, rz, s_pz.at[0], r_pz.at[0], z_dev(zl_n))
    pz.start()
    for cp in near_parts:
        cp.wait_recv()
    base_near = c * (10 * R)

    def near_step(i, carry):
        rows = pl.ds(pl.multiple_of(i * R, R), R)
        mine = part[:, pl.ds(pl.multiple_of(base_near + i * R, R), R), :]
        qsum[:, rows, :] = (mine + rnear[0, :, rows, :]) + (rnear[1, :, rows, :] + rnear[2, :, rows, :])
        return carry

    lax.fori_loop(0, 10, near_step, 0)
    pz.wait_recv()
    for i in range(10):
        rows = slice(i * R, (i + 1) * R)
        qsum[:, rows, :] = qsum[:, rows, :] + rz[:, rows, :]

    q_left = to_left(qsum.at[:, pl.ds(0, R), :], qhalo.at[1], s_q.at[0], r_q.at[1])
    q_right = to_right(qsum.at[:, pl.ds(7 * R, R), :], qhalo.at[0], s_q.at[1], r_q.at[0])
    send_sides([q_left], [q_right])

    @pl.when(has_left)
    def _():
        q_right.wait_recv()

    @pl.when(has_right)
    def _():
        q_left.wait_recv()

    def wide(ref, rows):
        return jnp.concatenate([ref[h, rows, :] for h in range(halves)], axis=1)

    every = slice(0, R)
    qs = [wide(qhalo.at[0], every)]
    qs += [wide(qsum, slice(l * R, (l + 1) * R)) for l in range(R)]
    qs += [wide(qhalo.at[1], every)]
    abs_vec = zero
    for l in range(R):
        v = qs[l + 1]
        before = jnp.where(y_first, wide(qsum, slice(8 * R + l, 8 * R + l + 1)), pltpu.roll(v, 1, 0))
        after = jnp.where(y_last, wide(qsum, slice(9 * R + l, 9 * R + l + 1)), pltpu.roll(v, R - 1, 0))
        value = (
            2.0 * v + qs[l] + qs[l + 2] + before + after
            + jnp.where(z_first, 0.0, z_prev(v)) + jnp.where(z_last, 0.0, z_next(v))
        )
        sens[l] = value
        abs_vec = abs_vec + jnp.abs(value)

    half = abs_vec[:, :128]
    for k in range(1, width // 128):
        half = half + abs_vec[:, k * 128:(k + 1) * 128]
    row = jnp.sum(half, axis=0, keepdims=True)
    sub1 = lax.broadcasted_iota(jnp.int32, (R, 128), 0)
    lane1 = lax.broadcasted_iota(jnp.int32, (R, 128), 1)
    mine_obj = (sub1 == 1) & (lane1 == c)
    now = jnp.where(sub1 == 0, row, jnp.where(mine_obj, obj_part, 0.0))

    stages = [
        (arx, s_ax, r_ax, XC, lambda d: {"case": c, "tile": x_tile(d)}),
        (ary, s_ay, r_ay, YD, lambda d: {"case": y_case(d), "tile": t}),
        (arz, s_az, r_az, z_n, z_dev),
    ]
    all_copies = []
    for i, (buf, ssem, rsem, count, dev) in enumerate(stages):
        msg[i] = now
        copies = []
        for d in range(1, count):
            cp = remote(msg.at[i], buf.at[d - 1], ssem.at[d - 1], rsem.at[d - 1], dev(d))
            cp.start()
            copies.append(cp)
        for cp in copies:
            cp.wait_recv()
        for d in range(1, count):
            now = now + buf[d - 1]
        all_copies += copies

    total_abs = jnp.sum(jnp.where(sub1 == 0, now, 0.0))
    scale = 1.0 / (total_abs / (grid_rows * R * R * width) + 1e-06)
    obj_out[...] = jnp.full(obj_out.shape, jnp.sum(jnp.where(mine_obj, now, 0.0)))
    for l in range(R):
        sens_out[l] = sens[l] * scale

    for cp in [z_copy, pz] + y_copies + yf_copies + far_parts + near_parts + all_copies:
        cp.wait_send()

    @pl.when(has_left)
    def _():
        for cp in [q_left] + halo_left + [left for left, _ in tile_copies]:
            cp.wait_send()

    @pl.when(has_right)
    def _():
        for cp in [q_right] + halo_right + [right for _, right in tile_copies]:
            cp.wait_send()


def body(density, heat_power, laser_mask, sink_mask):
    tiles = lax.axis_size("tile")
    rows, grid_y, width = sink_mask.shape
    planes = (R, R, width)
    halves = width // 128
    f32 = jnp.float32
    z_n = ZH * (tiles // XC)

    def vm(*shape):
        return pltpu.VMEM(shape, f32)

    def dma(*shape):
        return pltpu.SemaphoreType.DMA(shape)

    scratch = [
        vm(EXT, halves, grid_y, 128),
        vm(rows, halves, grid_y, 128),
        pltpu.VMEM((rows, halves, grid_y, 128), jnp.int32),
        pltpu.VMEM((EXT, halves, grid_y, 128), jnp.int32),
        vm(EXT, *planes),
        vm(EXT, *planes),
        vm(EXT, *planes),
    ] + [vm(EXT, *planes)] * 6 + [vm(2, EXT, *planes)] * 3 + [
        vm(halves, 8 * 10 * R, 128),
        vm(YD - 1, halves, 10 * R, 128),
        vm(YD - 1, halves, 10 * R, 128),
        vm(halves, 10 * R, 128),
        vm(halves, 10 * R, 128),
        vm(halves, 10 * R, 128),
        vm(2, halves, R, 128),
        vm(R, R, width),
        vm(3, R, 128),
        vm(XC - 1, R, 128),
        vm(YD - 1, R, 128),
        vm(z_n - 1, R, 128),
        dma(halves, 4),
        dma(YD - 1), dma(YD - 1),
        dma(1), dma(1),
        dma(YD - 1), dma(YD - 1),
        dma(2, 2 * YD), dma(2, 2 * YD),
        dma(4), dma(4),
        dma(2, YD - 1), dma(2, YD - 1),
        dma(1), dma(1),
        dma(2), dma(2),
        dma(XC - 1), dma(XC - 1),
        dma(YD - 1), dma(YD - 1),
        dma(z_n - 1), dma(z_n - 1),
    ]
    any_spec = pl.BlockSpec(memory_space=pl.ANY)
    vmem_spec = pl.BlockSpec(memory_space=pltpu.VMEM)
    sensitivity, objective = pl.pallas_call(
        functools.partial(kernel, tiles),
        out_shape=(
            jax.ShapeDtypeStruct(density.shape, f32),
            jax.ShapeDtypeStruct((1, 128), f32),
        ),
        in_specs=[any_spec] * 4,
        out_specs=(vmem_spec, vmem_spec),
        scratch_shapes=scratch,
        compiler_params=pltpu.CompilerParams(
            collective_id=0, has_side_effects=True, vmem_limit_bytes=48 * 1024 * 1024
        ),
    )(density, heat_power, laser_mask, sink_mask)
    return sensitivity, objective[0, :1]


def solution(mesh):
    return jax.shard_map(
        body,
        mesh=mesh,
        in_specs=(
            P("tile", "case", None),
            P("case", "tile", None, None),
            P("case", "tile", None, None),
            P("tile", None, None),
        ),
        out_specs=(P("tile", "case", None), P("case")),
        check_vma=False,
    )
```

time: 538 us -> 93.8 us (0.17)
  blocking collectives: 375 us -> 0 us
  Pallas kernels: 0 us -> 86.2 us
  starting transfers between devices: 74 us -> 0 us
  waiting for transfers between devices: 52.4 us -> 0 us
  other arithmetic: 18.8 us -> 0 us
  between operations: 15.5 us -> 1.82 us
    psum x2 -> x0, blocking collectives: 310 us -> none  [the longest x1 209 us: body(): objective_total = lax.psum(goal_derivative, 'tile')]
    pallas_call x0 -> x1, Pallas kernels: none -> 86.2 us  [body(): pl.pallas_call(functools.partial(kernel, tiles), out_shape=(jax.ShapeDtyp...]
    ppermute x28 -> x0, starting transfers between devices: 73.9 us -> none  [the longest x14 38.5 us: with_halo(): lax.ppermute(tail, axis, [(i, (i + 1) % count) for i in range(ends)])]
    all_gather x1 -> x0, blocking collectives: 64.9 us -> none  [body(): full_rows = lax.all_gather(density, 'case', axis=1, tiled=True)]
    ppermute x28 -> x0, waiting for transfers between devices: 52.4 us -> none  [the longest x14 52.3 us: with_halo(): lax.ppermute(head, axis, [((i + 1) % count, i) for i in range(ends)])]
    mul x38 -> x0, other arithmetic: 8.75 us -> none  [the longest x20 4.85 us: flux_sum(): face_cond * (lower_part(field, along) - upper_part(field, along))]
  transfers between devices with their start and end apart: 29 -> 0, of which waited for: 12 -> 0; matrix products, arithmetic and copies ran while one was open for 2% -> 0% of each run, Pallas kernels for 0% -> 0%
where the time goes in v1:
time: 93.8 us; the launch traced here: 92.6 us
  Pallas kernels  86.2 us (92%)
  local copies, waits for them, and re-layouts  4.59 us (5%)
  between operations  1.82 us (2%)
    pallas_call x1, Pallas kernels, body(): pl.pallas_call(functools.partial(kernel, tiles), out_shape=(jax.ShapeDtyp...  86.2 us
    unnamed x9, local copies, waits for them, and re-layouts  4.59 us

profile of v1, /device:TPU:1, one launch (start us, length us, event | category | flops | bytes accessed | tf_op | source)
XLA Modules:
  0.0 92.6 jit_solution(295744109018500338)
XLA Ops:
  0.6 0.0 copy-start
  0.6 1.0 %copy-done = f32[1,8,64,256]{3,2,1,0:T(8,128)S(1)} copy-done((f32[1,8,64,256]{3,2,1,0:T(8,128)S(1)}, f32[1,8,64,256]{3,2,1,0:T(8,128)}, u32[]{:S(2)}) %copy-start) | copy-done | bytes 524312
  1.7 0.0 copy-start.1
  1.7 1.0 %copy-done.1 = s32[1,8,64,256]{3,2,1,0:T(8,128)S(1)} copy-done((s32[1,8,64,256]{3,2,1,0:T(8,128)S(1)}, s32[1,8,64,256]{3,2,1,0:T(8,128)}, u32[]{:S(2)}) %copy-start.1) | copy-done | bytes 524312
  2.7 0.0 copy-start.2
  2.7 1.0 %copy-done.2 = s32[8,64,256]{2,1,0:T(8,128)S(1)} copy-done((s32[8,64,256]{2,1,0:T(8,128)S(1)}, s32[8,64,256]{2,1,0:T(8,128)}, u32[]{:S(2)}) %copy-start.2) | copy-done | bytes 524312
  3.8 0.0 copy-start.3
  3.8 0.8 copy-done.3
  4.6 86.2 %shard_map.59 = (f32[8,8,256]{2,1,0:T(8,128)S(1)}, f32[1,128]{1,0:T(1,128)S(1)}) custom-call(f32[8,8,256]{2,1,0:T(8,128)S(1)} %copy-done.3, f32[1,8,64,256]{3,2,1,0:T(8,128)S(1)} %copy-done, s32[1,8,64,256]{3,2,1,0:T(8,128)S(1)} %copy-done.1, s32[8,64,256]{2,1,0:T(8,128)S(1)} %copy-done.2), custom_call_target="tpu_custom_call" | custom-call | tf_op jit(solution)/shard_map/pallas_call | solution.py:566
  90.8 0.6 copy.8
Async XLA Ops:
  0.6 1.0 %copy-start = (f32[1,8,64,256]{3,2,1,0:T(8,128)S(1)}, f32[1,8,64,256]{3,2,1,0:T(8,128)}, u32[]{:S(2)}) copy-start(f32[1,8,64,256]{3,2,1,0:T(8,128)} %heat_in.1) | copy-start | bytes 1572868
  1.7 1.0 %copy-start.1 = (s32[1,8,64,256]{3,2,1,0:T(8,128)S(1)}, s32[1,8,64,256]{3,2,1,0:T(8,128)}, u32[]{:S(2)}) copy-start(s32[1,8,64,256]{3,2,1,0:T(8,128)} %laser_in.1) | copy-start | bytes 1572868
  2.7 1.0 %copy-start.2 = (s32[8,64,256]{2,1,0:T(8,128)S(1)}, s32[8,64,256]{2,1,0:T(8,128)}, u32[]{:S(2)}) copy-start(s32[8,64,256]{2,1,0:T(8,128)} %sink_in.1) | copy-start | bytes 1572868
  3.8 0.8 copy-start.3

commit v2 on v1

--- a/solution.py
+++ b/solution.py
@@ -18,6 +18,7 @@
 ZH = 2
 XC = 8
 R = 8
+HL = 4
 EXT = 3 * R
 
 
@@ -48,10 +49,10 @@
     tiles,
     dens_in, heat_in, laser_in, sink_in,
     sens_out, obj_out,
-    dens, heat, laser, sink, src, cond, wgt, kxm, kxp, kym, kyp, kzm, kzp, bias, ya, yb,
-    part, rfar, rnear, fsum, rz, qsum, qhalo, sens, msg, arx, ary, arz,
-    lsem, s_y, r_y, s_z, r_z, s_yf, r_yf, s_t, r_t, s_h, r_h, s_p, r_p, s_pz, r_pz, s_q, r_q,
-    s_ax, r_ax, s_ay, r_ay, s_az, r_az,
+    dens, relay, heat, laser, sink, src, cond, wgt, kxm, kxp, kym, kyp, kzm, kzp, bias, ya, yb,
+    part, rfar, rnear, fsum, rz, qsum, qhalo, sens, msg, arx, arz,
+    lsem, round_sem, s_zr, r_zr, s_y, r_y, s_z, r_z, s_yf, r_yf, s_t, r_t, s_tf, r_tf, s_h, r_h, s_p, r_p, s_pz, r_pz, s_q, r_q,
+    s_ax, r_ax, s_az, r_az,
 ):
     zl_n = tiles // XC
     z_n = ZH * zl_n
@@ -77,17 +78,19 @@
     def x_tile(d):
         return zl * XC + (xc + d) % XC
 
+    def plane_dev(k):
+        return {"case": y_case(k // XC), "tile": x_tile(k % XC)}
+
     barrier = pltpu.get_barrier_semaphore()
 
     def greet(dev):
         pl.semaphore_signal(barrier, inc=1, device_id=dev, device_id_type=MESH)
 
-    for d in range(1, z_n):
-        greet(z_dev(d))
-    for d in range(1, YD):
-        greet({"case": y_case(d), "tile": t})
-    for d in range(1, XC):
-        greet({"case": c, "tile": x_tile(d)})
+    met = [z_dev(d) for d in (1, 2, 4, z_n - 1, z_n - 2, z_n - 4)]
+    met += [{"case": y_case(d), "tile": t} for d in range(1, YD)]
+    met += [{"case": c, "tile": x_tile(d)} for d in range(1, XC)]
+    for dev in met:
+        greet(dev)
 
     @pl.when(has_left)
     def _():
@@ -125,10 +128,6 @@
         sink[2 * R:3 * R - 2] = jnp.zeros((R - 2,) + sink.shape[1:], jnp.int32)
         qhalo[1] = jnp.zeros(qhalo.shape[1:], jnp.float32)
 
-    for k in range(3):
-        for h in range(halves):
-            loads[h][k].wait()
-
     def row_load(ref, l, j):
         return jnp.concatenate([ref[l, h, pl.ds(j, R, stride=R), :] for h in range(halves)], axis=1)
 
@@ -137,13 +136,31 @@
             src[l + R, j] = row_load(heat, l, j) * row_load(laser, l, j).astype(jnp.float32)
         return carry
 
-    lax.fori_loop(0, R, make_source, 0)
-
-    for h in range(halves):
-        loads[h][3].wait()
     pl.semaphore_wait(
-        barrier, (z_n - 1) + (YD - 1) + (XC - 1) + has_left.astype(jnp.int32) + has_right.astype(jnp.int32)
+        barrier, len(met) + has_left.astype(jnp.int32) + has_right.astype(jnp.int32)
     )
+
+    sends = []
+
+    def drain():
+        for guard, group in ((None, []), (has_left, []), (has_right, [])):
+            group = [cp for g, cp in sends if g is guard]
+            if not group:
+                continue
+
+            def wait_all(group=group):
+                for cp in group:
+                    cp.wait_send()
+
+            if guard is None:
+                wait_all()
+            else:
+                pl.when(guard)(wait_all)
+
+    def push(cp):
+        cp.start()
+        sends.append((None, cp))
+        return cp
 
     def remote(a, b, ssem, rsem, dev):
         return pltpu.make_async_remote_copy(
@@ -156,14 +173,34 @@
     def to_right(a, b, ssem, rsem):
         return remote(a, b, ssem, rsem, {"case": c, "tile": jnp.minimum(t + 1, tiles - 1)})
 
-    own = dens.at[pl.ds(R, R), :, slab, :]
-    z_copy = remote(own, own, s_z.at[0], r_z.at[0], z_dev(zl_n))
-    z_copy.start()
+    def piece(base, k, rows):
+        return dens.at[pl.ds(base + (k // halves) * HL, HL), k % halves, rows, :]
+
+    def piece_in(k):
+        return dens_in.at[pl.ds((k // halves) * HL, HL), :, pl.ds((k % halves) * 128, 128)]
+
+    pieces = halves * R // HL
+    quarter = z_n // 4
+    column = xc // 2
+    via = []
+    for k in range(pieces):
+        way = quarter if k < pieces // 2 else z_n - quarter
+        way = jnp.where(column == 0, quarter, way)
+        via.append(jnp.where(column == XC // 2 - 1, z_n - quarter, way))
+    for k in range(pieces):
+        push(remote(piece_in(k), relay.at[k], s_zr.at[k], r_zr.at[k], z_dev(via[k])))
     y_copies = []
     for d in range(1, YD):
-        cp = remote(own, own, s_y.at[d - 1], r_y.at[d - 1], {"case": y_case(d), "tile": t})
-        cp.start()
-        y_copies.append(cp)
+        to = {"case": y_case(d), "tile": t}
+        y_copies.append([
+            push(remote(piece_in(k), piece(R, k, slab), s_y.at[d - 1, k], r_y.at[d - 1, k], to))
+            for k in range(pieces)
+        ])
+
+    for dev in met:
+        pl.semaphore_signal(round_sem.at[0], inc=1, device_id=dev, device_id_type=MESH)
+    for h in range(halves):
+        loads[h][3].wait()
 
     halo_left = [
         to_left(src.at[pl.ds(R, R - 2)], src.at[pl.ds(2 * R, R - 2)], s_h.at[0], r_h.at[1]),
@@ -185,7 +222,15 @@
             for cp in right:
                 cp.start()
 
-    send_sides(halo_left, halo_right)
+        sends.extend((has_left, cp) for cp in left)
+        sends.extend((has_right, cp) for cp in right)
+
+    send_sides(halo_left[1:], halo_right[1:])
+    for k in range(3):
+        for h in range(halves):
+            loads[h][k].wait()
+    lax.fori_loop(0, R, make_source, 0)
+    send_sides(halo_left[:1], halo_right[:1])
 
     def slab_of(case):
         return pl.ds(pl.multiple_of(case * R, R), R)
@@ -193,30 +238,63 @@
     tile_copies = []
 
     def forward(case, order):
-        here = dens.at[pl.ds(R, R), :, slab_of(case), :]
-        left = to_left(here, dens.at[pl.ds(2 * R, R), :, slab_of(case), :], s_t.at[0, order], r_t.at[1, order])
-        right = to_right(here, dens.at[pl.ds(0, R), :, slab_of(case), :], s_t.at[1, order], r_t.at[0, order])
+        rows = slab_of(case)
+        here = dens.at[pl.ds(R, R), :, rows, :]
+        left = to_left(here, dens.at[pl.ds(2 * R, R), :, rows, :], s_t.at[0, order], r_t.at[1, order])
+        right = to_right(here, dens.at[pl.ds(0, R), :, rows, :], s_t.at[1, order], r_t.at[0, order])
         send_sides([left], [right])
         tile_copies.append((left, right))
 
+    def forward_piece(case, order, k):
+        rows = slab_of(case)
+        here = piece(R, k, rows)
+        left = to_left(here, piece(2 * R, k, rows), s_tf.at[0, order, k], r_tf.at[1, order, k])
+        right = to_right(here, piece(0, k, rows), s_tf.at[1, order, k], r_tf.at[0, order, k])
+        send_sides([left], [right])
+        tile_copies.append((left, right))
+
     forward(c, 0)
     for d in range(1, YD):
-        y_copies[d - 1].wait_recv()
+        for cp in y_copies[d - 1]:
+            cp.wait_recv()
         forward(zh * YD + (yy + YD - d) % YD, d)
 
-    z_copy.wait_recv()
+    z_copies = []
+    for k in range(pieces):
+        into = relay.at[k]
+        remote(into, into, s_zr.at[k], r_zr.at[k], z_dev(via[k])).wait_recv()
+        origin = z_dev(z_n - via[k])["case"]
+        z_copies.append(
+            push(remote(into, piece(R, k, slab_of(origin)), s_z.at[k], r_z.at[k], z_dev(via[k])))
+        )
+    pl.semaphore_wait(round_sem.at[0], len(met))
+    for dev in met:
+        pl.semaphore_signal(round_sem.at[1], inc=1, device_id=dev, device_id_type=MESH)
+
     far = (1 - zh) * YD
     far_case = far + yy
-    far_ref = dens.at[pl.ds(R, R), :, slab_of(far_case), :]
     yf_copies = []
-    for d in range(1, YD):
-        cp = remote(far_ref, far_ref, s_yf.at[d - 1], r_yf.at[d - 1], {"case": y_case(d), "tile": t})
-        cp.start()
-        yf_copies.append(cp)
-    forward(far_case, YD)
-    for d in range(1, YD):
-        yf_copies[d - 1].wait_recv()
-        forward(far + (yy + YD - d) % YD, YD + d)
+
+    def cross(k):
+        z_copies[k].wait_recv()
+        here = piece(R, k, slab_of(far_case))
+        yf_copies.append([
+            push(remote(here, here, s_yf.at[d - 1, k], r_yf.at[d - 1, k], {"case": y_case(d), "tile": t}))
+            for d in range(1, YD)
+        ])
+        forward_piece(far_case, 0, k)
+
+    def spread(k):
+        for d in range(1, YD):
+            yf_copies[k][d - 1].wait_recv()
+            forward_piece(far + (yy + YD - d) % YD, d, k)
+
+    for k in range(pieces - 1):
+        cross(k)
+    spread(0)
+    cross(pieces - 1)
+    for k in range(1, pieces):
+        spread(k)
 
     @pl.when(has_left)
     def _():
@@ -247,6 +325,18 @@
 
     def z_next(v):
         return pltpu.roll(v, width - 1, 1)
+
+    lane_h = lax.broadcasted_iota(jnp.int32, (R, 128), 1)
+
+    def z_from_prev(v):
+        turned = [pltpu.roll(v[:, h * 128:(h + 1) * 128], 1, 1) for h in range(halves)]
+        out = turned[:1] + [jnp.where(lane_h == 0, turned[h - 1], turned[h]) for h in range(1, halves)]
+        return jnp.concatenate(out, axis=1)
+
+    def z_from_next(v):
+        turned = [pltpu.roll(v[:, h * 128:(h + 1) * 128], 127, 1) for h in range(halves)]
+        out = [jnp.where(lane_h == 127, turned[h + 1], turned[h]) for h in range(halves - 1)] + turned[-1:]
+        return jnp.concatenate(out, axis=1)
 
     def around(planes, j):
         before = planes[j - 1] if j > 0 else pltpu.roll(planes[R - 1], 1, 0)
@@ -283,7 +373,7 @@
             wgt[e, j] = (-1.5 * (1.0 - low_cond) * LEAD * LEAD) * sq * inv
         return carry
 
-    lax.fori_loop(1, EXT - 1, physical_step, 0)
+    lax.fori_loop(1, EXT - 1, physical_step, 0, unroll=2)
 
     def inside(g):
         return (g >= 0) & (g < grid_rows)
@@ -320,7 +410,7 @@
             bias[1, e, j] = jnp.where(source > 0.0, scale, 0.0)
         return carry
 
-    lax.fori_loop(2, EXT - 2, face_step, 0)
+    lax.fori_loop(2, EXT - 2, face_step, 0, unroll=2)
 
     def sweep(n, y_in, y_out):
         ratio = COEF[SWEEPS - 2 - n] / LEAD
@@ -337,12 +427,12 @@
                     acc = acc + ks[1] * y_in[f, e + 1, j]
                     acc = acc + ks[2] * before
                     acc = acc + ks[3] * after
-                    acc = acc + ks[4] * z_prev(v)
-                    acc = acc + ks[5] * z_next(v)
+                    acc = acc + ks[4] * z_from_prev(v)
+                    acc = acc + ks[5] * z_from_next(v)
                     y_out[f, e, j] = acc
             return carry
 
-        lax.fori_loop(3 + n, EXT - 3 - n, step, 0)
+        lax.fori_loop(3 + n, EXT - 3 - n, step, 0, unroll=2)
 
     bufs = [bias, ya, yb, ya, yb, ya]
     for n in range(SWEEPS - 1):
@@ -385,54 +475,50 @@
             total = total + jnp.where(src[e, j] > 0.0, p, 0.0)
         return total
 
-    obj_vec = lax.fori_loop(R, 2 * R, product_step, zero)
+    obj_vec = lax.fori_loop(R, 2 * R, product_step, zero, unroll=2)
 
     def block(case):
         return pl.ds(pl.multiple_of(case * (10 * R), 10 * R), 10 * R)
 
-    far_parts = []
-    near_parts = []
-    for d in range(1, YD):
-        dest = (yy + d) % YD
-        cp = remote(part.at[:, block(far + dest)], rfar.at[d - 1], s_p.at[0, d - 1], r_p.at[0, d - 1],
-                    {"case": y_case(d), "tile": t})
-        cp.start()
-        far_parts.append(cp)
-    for d in range(1, YD):
-        dest = (yy + d) % YD
-        cp = remote(part.at[:, block(zh * YD + dest)], rnear.at[d - 1], s_p.at[1, d - 1], r_p.at[1, d - 1],
-                    {"case": y_case(d), "tile": t})
-        cp.start()
-        near_parts.append(cp)
-    obj_part = LEAD * jnp.sum(obj_vec)
-    for cp in far_parts:
-        cp.wait_recv()
-    base_far = far_case * (10 * R)
-
-    def far_step(i, carry):
-        rows = pl.ds(pl.multiple_of(i * R, R), R)
-        mine = part[:, pl.ds(pl.multiple_of(base_far + i * R, R), R), :]
-        fsum[:, rows, :] = (mine + rfar[0, :, rows, :]) + (rfar[1, :, rows, :] + rfar[2, :, rows, :])
-        return carry
-
-    lax.fori_loop(0, 10, far_step, 0)
-    pz = remote(fsum, rz, s_pz.at[0], r_pz.at[0], z_dev(zl_n))
-    pz.start()
-    for cp in near_parts:
-        cp.wait_recv()
-    base_near = c * (10 * R)
-
-    def near_step(i, carry):
-        rows = pl.ds(pl.multiple_of(i * R, R), R)
-        mine = part[:, pl.ds(pl.multiple_of(base_near + i * R, R), R), :]
-        qsum[:, rows, :] = (mine + rnear[0, :, rows, :]) + (rnear[1, :, rows, :] + rnear[2, :, rows, :])
-        return carry
-
-    lax.fori_loop(0, 10, near_step, 0)
-    pz.wait_recv()
-    for i in range(10):
-        rows = slice(i * R, (i + 1) * R)
-        qsum[:, rows, :] = qsum[:, rows, :] + rz[:, rows, :]
+    def y_parts(side, dest_base, buf):
+        return [
+            [
+                push(remote(
+                    part.at[h, block(dest_base + (yy + d) % YD)], buf.at[d - 1, h],
+                    s_p.at[side, d - 1, h], r_p.at[side, d - 1, h], {"case": y_case(d), "tile": t},
+                ))
+                for d in range(1, YD)
+            ]
+            for h in range(halves)
+        ]
+
+    def add_parts(h, case, buf, out):
+        base = case * (10 * R)
+
+        def step(i, carry):
+            rows = pl.ds(pl.multiple_of(i * R, R), R)
+            mine = part[h, pl.ds(pl.multiple_of(base + i * R, R), R), :]
+            out[h, rows, :] = (mine + buf[0, h, rows, :]) + (buf[1, h, rows, :] + buf[2, h, rows, :])
+            return carry
+
+        lax.fori_loop(0, 10, step, 0, unroll=5)
+
+    far_parts = y_parts(0, far, rfar)
+    obj_part = LEAD * jnp.sum(obj_vec, axis=(0, 1), keepdims=True)
+    crossing = []
+    for h in range(halves):
+        for cp in far_parts[h]:
+            cp.wait_recv()
+        add_parts(h, far_case, rfar, fsum)
+        crossing.append(push(remote(fsum.at[h], rz.at[h], s_pz.at[h], r_pz.at[h], z_dev(zl_n))))
+    near_parts = y_parts(1, zh * YD, rnear)
+    for h in range(halves):
+        for cp in near_parts[h]:
+            cp.wait_recv()
+        add_parts(h, c, rnear, qsum)
+    for h in range(halves):
+        crossing[h].wait_recv()
+        qsum[h] = qsum[h] + rz[h]
 
     q_left = to_left(qsum.at[:, pl.ds(0, R), :], qhalo.at[1], s_q.at[0], r_q.at[1])
     q_right = to_right(qsum.at[:, pl.ds(7 * R, R), :], qhalo.at[0], s_q.at[1], r_q.at[0])
@@ -465,52 +551,28 @@
         sens[l] = value
         abs_vec = abs_vec + jnp.abs(value)
 
-    half = abs_vec[:, :128]
-    for k in range(1, width // 128):
-        half = half + abs_vec[:, k * 128:(k + 1) * 128]
-    row = jnp.sum(half, axis=0, keepdims=True)
-    sub1 = lax.broadcasted_iota(jnp.int32, (R, 128), 0)
-    lane1 = lax.broadcasted_iota(jnp.int32, (R, 128), 1)
-    mine_obj = (sub1 == 1) & (lane1 == c)
-    now = jnp.where(sub1 == 0, row, jnp.where(mine_obj, obj_part, 0.0))
-
-    stages = [
-        (arx, s_ax, r_ax, XC, lambda d: {"case": c, "tile": x_tile(d)}),
-        (ary, s_ay, r_ay, YD, lambda d: {"case": y_case(d), "tile": t}),
-        (arz, s_az, r_az, z_n, z_dev),
-    ]
-    all_copies = []
-    for i, (buf, ssem, rsem, count, dev) in enumerate(stages):
+    pl.semaphore_wait(round_sem.at[1], len(met))
+    lane1 = lax.broadcasted_iota(jnp.int32, (1, 128), 1)
+    now = jnp.where(lane1 == 8, jnp.sum(abs_vec, axis=(0, 1), keepdims=True), jnp.where(lane1 == c, obj_part, 0.0))
+    for i, (buf, ssem, rsem, count, dev) in enumerate(
+        [(arx, s_ax, r_ax, YD * XC, plane_dev), (arz, s_az, r_az, z_n, z_dev)]
+    ):
         msg[i] = now
-        copies = []
-        for d in range(1, count):
-            cp = remote(msg.at[i], buf.at[d - 1], ssem.at[d - 1], rsem.at[d - 1], dev(d))
-            cp.start()
-            copies.append(cp)
+        copies = [
+            push(remote(msg.at[i], buf.at[k - 1], ssem.at[k - 1], rsem.at[k - 1], dev(k))) for k in range(1, count)
+        ]
         for cp in copies:
             cp.wait_recv()
-        for d in range(1, count):
-            now = now + buf[d - 1]
-        all_copies += copies
-
-    total_abs = jnp.sum(jnp.where(sub1 == 0, now, 0.0))
+        for k in range(1, count):
+            now = now + buf[k - 1]
+
+    total_abs = jnp.sum(jnp.where(lane1 == 8, now, 0.0), axis=(0, 1), keepdims=True)
     scale = 1.0 / (total_abs / (grid_rows * R * R * width) + 1e-06)
-    obj_out[...] = jnp.full(obj_out.shape, jnp.sum(jnp.where(mine_obj, now, 0.0)))
+    obj_out[...] = jnp.zeros_like(obj_out) + jnp.sum(jnp.where(lane1 == c, now, 0.0), axis=(0, 1), keepdims=True)
     for l in range(R):
         sens_out[l] = sens[l] * scale
 
-    for cp in [z_copy, pz] + y_copies + yf_copies + far_parts + near_parts + all_copies:
-        cp.wait_send()
-
-    @pl.when(has_left)
-    def _():
-        for cp in [q_left] + halo_left + [left for left, _ in tile_copies]:
-            cp.wait_send()
-
-    @pl.when(has_right)
-    def _():
-        for cp in [q_right] + halo_right + [right for _, right in tile_copies]:
-            cp.wait_send()
+    drain()
 
 
 def body(density, heat_power, laser_mask, sink_mask):
@@ -518,6 +580,7 @@
     rows, grid_y, width = sink_mask.shape
     planes = (R, R, width)
     halves = width // 128
+    pieces = halves * R // HL
     f32 = jnp.float32
     z_n = ZH * (tiles // XC)
 
@@ -529,6 +592,7 @@
 
     scratch = [
         vm(EXT, halves, grid_y, 128),
+        vm(pieces, HL, R, 128),
         vm(rows, halves, grid_y, 128),
         pltpu.VMEM((rows, halves, grid_y, 128), jnp.int32),
         pltpu.VMEM((EXT, halves, grid_y, 128), jnp.int32),
@@ -544,21 +608,22 @@
         vm(halves, 10 * R, 128),
         vm(2, halves, R, 128),
         vm(R, R, width),
-        vm(3, R, 128),
-        vm(XC - 1, R, 128),
-        vm(YD - 1, R, 128),
-        vm(z_n - 1, R, 128),
+        vm(2, 1, 128),
+        vm(YD * XC - 1, 1, 128),
+        vm(z_n - 1, 1, 128),
         dma(halves, 4),
-        dma(YD - 1), dma(YD - 1),
-        dma(1), dma(1),
-        dma(YD - 1), dma(YD - 1),
-        dma(2, 2 * YD), dma(2, 2 * YD),
+        pltpu.SemaphoreType.REGULAR((2,)),
+        dma(pieces), dma(pieces),
+        dma(YD - 1, pieces), dma(YD - 1, pieces),
+        dma(pieces), dma(pieces),
+        dma(YD - 1, pieces), dma(YD - 1, pieces),
+        dma(2, YD), dma(2, YD),
+        dma(2, YD, pieces), dma(2, YD, pieces),
         dma(4), dma(4),
-        dma(2, YD - 1), dma(2, YD - 1),
-        dma(1), dma(1),
+        dma(2, YD - 1, halves), dma(2, YD - 1, halves),
+        dma(halves), dma(halves),
         dma(2), dma(2),
-        dma(XC - 1), dma(XC - 1),
-        dma(YD - 1), dma(YD - 1),
+        dma(YD * XC - 1), dma(YD * XC - 1),
         dma(z_n - 1), dma(z_n - 1),
     ]
     any_spec = pl.BlockSpec(memory_space=pl.ANY)
@@ -573,7 +638,7 @@
         out_specs=(vmem_spec, vmem_spec),
         scratch_shapes=scratch,
         compiler_params=pltpu.CompilerParams(
-            collective_id=0, has_side_effects=True, vmem_limit_bytes=48 * 1024 * 1024
+            collective_id=0, has_side_effects=True, vmem_limit_bytes=56150000
         ),
     )(density, heat_power, laser_mask, sink_mask)
     return sensitivity, objective[0, :1]

time: 93.8 us -> 84.3 us (0.90); the launches traced: 92.6 us -> 84.1 us
  Pallas kernels: 86.2 us -> 80.8 us
  local copies, waits for them, and re-layouts: 4.59 us -> 1.46 us
    pallas_call x1, Pallas kernels: 86.2 us -> 80.8 us  [body(): pl.pallas_call(functools.partial(kernel, tiles), out_shape=(jax.ShapeDtyp...]
    unnamed x9 -> x3, local copies, waits for them, and re-layouts: 4.59 us -> 1.46 us
where the time goes in v2:
time: 84.3 us; the launch traced here: 84.1 us
  Pallas kernels  80.8 us (96%)
  between operations  1.81 us (2%)
  local copies, waits for them, and re-layouts  1.46 us (2%)
    pallas_call x1, Pallas kernels, body(): pl.pallas_call(functools.partial(kernel, tiles), out_shape=(jax.ShapeDtyp...  80.8 us

profile of v2, /device:TPU:1, one launch (start us, length us, event | category | flops | bytes accessed | tf_op | source)
XLA Modules:
  0.0 84.1 jit_solution(12166171099304301990)
XLA Ops:
  0.6 0.0 copy-start
  0.6 0.8 copy-done
  1.5 80.8 %shard_map.59 = (f32[8,8,256]{2,1,0:T(8,128)S(1)}, f32[1,128]{1,0:T(1,128)S(1)}) custom-call(f32[8,8,256]{2,1,0:T(8,128)S(1)} %copy-done, f32[1,8,64,256]{3,2,1,0:T(8,128)} %heat_in.1, s32[1,8,64,256]{3,2,1,0:T(8,128)} %laser_in.1, s32[8,64,256]{2,1,0:T(8,128)} %sink_in.1), custom_call_target="tpu_custom_call" | custom-call | tf_op jit(solution)/shard_map/pallas_call | solution.py:631
  82.3 0.6 copy.8
Async XLA Ops:
  0.6 0.8 copy-start

commit v3 on v2

--- a/solution.py
+++ b/solution.py
@@ -14,11 +14,13 @@
 eig_high = 2.0
 
 MESH = pl.DeviceIdType.MESH
+UNROLL = (6, 4, 7, 6, 5)
 YD = 4
 ZH = 2
 XC = 8
 R = 8
 HL = 4
+RL = 5
 EXT = 3 * R
 
 
@@ -49,11 +51,12 @@
     tiles,
     dens_in, heat_in, laser_in, sink_in,
     sens_out, obj_out,
-    dens, relay, heat, laser, sink, src, cond, wgt, kxm, kxp, kym, kyp, kzm, kzp, bias, ya, yb,
-    part, rfar, rnear, fsum, rz, qsum, qhalo, sens, msg, arx, arz,
-    lsem, round_sem, s_zr, r_zr, s_y, r_y, s_z, r_z, s_yf, r_yf, s_t, r_t, s_tf, r_tf, s_h, r_h, s_p, r_p, s_pz, r_pz, s_q, r_q,
-    s_ax, r_ax, s_az, r_az,
+    dens, relay, heat, laser, sink, src, wgt, fin, *rest,
 ):
+    near_set, far_set, rest = rest[:12], rest[12:24], rest[24:]
+    (
+        part, rfar, rnear, fsum, rz, nsum, nhalo, rhalo, sens, msg, arx, arz, lsem, round_sem, s_zr, r_zr, s_y, r_y, s_z, r_z, s_yf, r_yf, s_t, r_t, s_tf, r_tf, s_h, r_h, s_p, r_p, s_pz, r_pz, s_q, r_q, s_ax, r_ax, s_az, r_az,
+    ) = rest
     zl_n = tiles // XC
     z_n = ZH * zl_n
     c = lax.axis_index("case")
@@ -119,21 +122,22 @@
         dens[0:R] = jnp.zeros((R,) + dens.shape[1:], jnp.float32)
         src[2:R] = jnp.zeros((R - 2,) + src.shape[1:], jnp.float32)
         sink[2:R] = jnp.zeros((R - 2,) + sink.shape[1:], jnp.int32)
-        qhalo[0] = jnp.zeros(qhalo.shape[1:], jnp.float32)
+        nhalo[0] = jnp.zeros(nhalo.shape[1:], jnp.float32)
+        rhalo[0] = jnp.zeros(rhalo.shape[1:], jnp.float32)
 
     @pl.when(t == tiles - 1)
     def _():
         dens[2 * R:] = jnp.zeros((R,) + dens.shape[1:], jnp.float32)
         src[2 * R:3 * R - 2] = jnp.zeros((R - 2,) + src.shape[1:], jnp.float32)
         sink[2 * R:3 * R - 2] = jnp.zeros((R - 2,) + sink.shape[1:], jnp.int32)
-        qhalo[1] = jnp.zeros(qhalo.shape[1:], jnp.float32)
-
-    def row_load(ref, l, j):
-        return jnp.concatenate([ref[l, h, pl.ds(j, R, stride=R), :] for h in range(halves)], axis=1)
+        nhalo[1] = jnp.zeros(nhalo.shape[1:], jnp.float32)
+        rhalo[1] = jnp.zeros(rhalo.shape[1:], jnp.float32)
 
     def make_source(l, carry):
         for j in range(R):
-            src[l + R, j] = row_load(heat, l, j) * row_load(laser, l, j).astype(jnp.float32)
+            for h in range(halves):
+                rows = pl.ds(j * R, R)
+                src[l + R, h, rows, :] = heat[l, h, rows, :] * laser[l, h, rows, :].astype(jnp.float32)
         return carry
 
     pl.semaphore_wait(
@@ -230,7 +234,6 @@
         for h in range(halves):
             loads[h][k].wait()
     lax.fori_loop(0, R, make_source, 0)
-    send_sides(halo_left[:1], halo_right[:1])
 
     def slab_of(case):
         return pl.ds(pl.multiple_of(case * R, R), R)
@@ -258,6 +261,8 @@
         for cp in y_copies[d - 1]:
             cp.wait_recv()
         forward(zh * YD + (yy + YD - d) % YD, d)
+
+    send_sides(halo_left[:1], halo_right[:1])
 
     z_copies = []
     for k in range(pieces):
@@ -278,37 +283,33 @@
     def cross(k):
         z_copies[k].wait_recv()
         here = piece(R, k, slab_of(far_case))
-        yf_copies.append([
-            push(remote(here, here, s_yf.at[d - 1, k], r_yf.at[d - 1, k], {"case": y_case(d), "tile": t}))
-            for d in range(1, YD)
-        ])
+        yf_copies.append({
+            d: push(remote(here, here, s_yf.at[d - 1, k], r_yf.at[d - 1, k], {"case": y_case(d), "tile": t}))
+            for d in (2, 1, 3)
+        })
         forward_piece(far_case, 0, k)
 
     def spread(k):
-        for d in range(1, YD):
-            yf_copies[k][d - 1].wait_recv()
+        for d in (1, 3, 2):
+            yf_copies[k][d].wait_recv()
             forward_piece(far + (yy + YD - d) % YD, d, k)
 
-    for k in range(pieces - 1):
+    for k in range(pieces):
         cross(k)
-    spread(0)
-    cross(pieces - 1)
-    for k in range(1, pieces):
-        spread(k)
-
-    @pl.when(has_left)
-    def _():
-        for left, right in tile_copies:
-            right.wait_recv()
-        for cp in halo_right:
-            cp.wait_recv()
-
-    @pl.when(has_right)
-    def _():
-        for left, right in tile_copies:
-            left.wait_recv()
-        for cp in halo_left:
-            cp.wait_recv()
+
+    def wait_sides(left, right):
+        @pl.when(has_left)
+        def _():
+            for cp in right:
+                cp.wait_recv()
+
+        @pl.when(has_right)
+        def _():
+            for cp in left:
+                cp.wait_recv()
+
+    def wait_tiles(pairs):
+        wait_sides([left for left, _ in pairs], [right for _, right in pairs])
 
     lane = lax.broadcasted_iota(jnp.int32, (R, width), 1)
     sub = lax.broadcasted_iota(jnp.int32, (R, width), 0)
@@ -338,161 +339,213 @@
         out = [jnp.where(lane_h == 127, turned[h + 1], turned[h]) for h in range(halves - 1)] + turned[-1:]
         return jnp.concatenate(out, axis=1)
 
-    def around(planes, j):
-        before = planes[j - 1] if j > 0 else pltpu.roll(planes[R - 1], 1, 0)
-        after = planes[j + 1] if j < R - 1 else pltpu.roll(planes[0], R - 1, 0)
-        return before, after
-
     def flag(cond_):
         return cond_.astype(jnp.float32)
 
-    def physical_step(e, carry):
+    def inside(g):
+        return (g >= 0) & (g < grid_rows)
+
+    class Rows:
+        def __init__(self, base, count, refs, near=None):
+            self.base, self.count, self.near = base, count, near
+            self.cond, *self.ks = refs[:7]
+            self.ys = refs[7:]
+            self.low = 0.0 if near is None else flag(zh == 0)
+            self.high = 0.0 if near is None else flag(zh == 1)
+
+        def rows(self, j):
+            return pl.ds(self.base + j, R, stride=self.count)
+
+        def load(self, ref, e, j):
+            return jnp.concatenate([ref[e, h, self.rows(j), :] for h in range(halves)], axis=1)
+
+        def store(self, ref, e, j, value):
+            for h in range(halves):
+                ref[e, h, self.rows(j), :] = value[:, h * 128:(h + 1) * 128]
+
+        def around(self, planes, outer=None):
+            first = pltpu.roll(planes[-1], 1, 0)
+            last = pltpu.roll(planes[0], R - 1, 0)
+            if outer is not None:
+                first = jnp.where(y_first, outer[0], first)
+                last = jnp.where(y_last, outer[1], last)
+            return [first] + planes[:-1], planes[1:] + [last]
+
+        def outer(self, get):
+            if self.near is None:
+                return None
+            return get(self.near, YD - 1)[5:6], get(self.near, 0)[2:3]
+
+    def physical_step(e, part_):
         g = t * R - R + e
         nx = 2.0 + flag(g > 0) + flag(g < grid_rows - 1)
         nyz = nx + jnp.where(z_first | z_last, 1.0, 2.0)
-        planes = [row_load(dens, e, j) for j in range(R)]
-        for j in range(R):
-            v = planes[j]
-            before, after = around(planes, j)
-            ny = jnp.full((R, width), 2.0)
+        planes = [part_.load(dens, e, j) for j in range(part_.count)]
+        outside = None
+        if part_.near is not None:
+            outside = [
+                jnp.concatenate([dens[e, h, y:y + 1, :] for h in range(halves)], axis=1)
+                for y in (3 * R - 1, 5 * R)
+            ]
+        befores, afters = part_.around(planes, outside)
+        for j in range(part_.count):
+            v, before, after = planes[j], befores[j], afters[j]
+            ny = 2.0
             if j == 0:
-                before = jnp.where(y_first, 0.0, before)
-                ny = jnp.where(y_first, 1.0, 2.0)
-            if j == R - 1:
-                after = jnp.where(y_last, 0.0, after)
-                ny = jnp.where(y_last, 1.0, 2.0)
+                has = jnp.where(y_first, part_.low, 1.0)
+                before = before * has
+                ny = 1.0 + has
+            if j == part_.count - 1:
+                has = jnp.where(y_last, part_.high, 1.0)
+                after = after * has
+                ny = 1.0 + has
             total = (
-                2.0 * v + row_load(dens, e - 1, j) + row_load(dens, e + 1, j)
-                + before + after
+                2.0 * v + part_.load(dens, e - 1, j) + part_.load(dens, e + 1, j) + before + after
                 + jnp.where(z_first, 0.0, z_prev(v)) + jnp.where(z_last, 0.0, z_next(v))
             )
             inv = 1.0 / (nyz + ny)
             phys = total * inv
             sq = phys * phys
-            cond[e, j] = low_cond + (1.0 - low_cond) * (sq * phys)
-            wgt[e, j] = (-1.5 * (1.0 - low_cond) * LEAD * LEAD) * sq * inv
-        return carry
-
-    lax.fori_loop(1, EXT - 1, physical_step, 0, unroll=2)
-
-    def inside(g):
-        return (g >= 0) & (g < grid_rows)
-
-    def face_step(e, carry):
+            part_.cond[e, j] = low_cond + (1.0 - low_cond) * (sq * phys)
+            part_.store(wgt, e, j, (-1.5 * (1.0 - low_cond) * LEAD * LEAD) * sq * inv)
+
+    def face_step(e, part_):
         g = t * R - R + e
         vm = 0.5 * flag(inside(g - 1) & inside(g))
         vp = 0.5 * flag(inside(g) & inside(g + 1))
-        planes = [cond[e, j] for j in range(R)]
-        for j in range(R):
+        cond = part_.cond
+        planes = [cond[e, j] for j in range(part_.count)]
+        befores, afters = part_.around(planes, part_.outer(lambda near, j: near.cond[e, j]))
+        for j in range(part_.count):
             v = planes[j]
-            before, after = around(planes, j)
             f_xm = vm * (cond[e - 1, j] + v)
             f_xp = vp * (cond[e + 1, j] + v)
-            f_ym = 0.5 * (before + v)
-            f_yp = 0.5 * (after + v)
+            f_ym = 0.5 * (befores[j] + v)
+            f_yp = 0.5 * (afters[j] + v)
             if j == 0:
-                f_ym = jnp.where(y_first, 0.0, f_ym)
-            if j == R - 1:
-                f_yp = jnp.where(y_last, 0.0, f_yp)
+                f_ym = f_ym * jnp.where(y_first, part_.low, 1.0)
+            if j == part_.count - 1:
+                f_yp = f_yp * jnp.where(y_last, part_.high, 1.0)
             f_zm = jnp.where(z_first, 0.0, 0.5 * (z_prev(v) + v))
             f_zp = jnp.where(z_last, 0.0, 0.5 * (z_next(v) + v))
             diag = heat_loss + f_xm + f_xp + f_ym + f_yp + f_zm + f_zp
-            free = jnp.where(row_load(sink, e, j) == 0, 1.0, 0.0)
+            free = jnp.where(part_.load(sink, e, j) == 0, 1.0, 0.0)
             scale = free / diag
-            kxm[e, j] = scale * f_xm
-            kxp[e, j] = scale * f_xp
-            kym[e, j] = scale * f_ym
-            kyp[e, j] = scale * f_yp
-            kzm[e, j] = scale * f_zm
-            kzp[e, j] = scale * f_zp
-            source = src[e, j]
-            bias[0, e, j] = scale * source
-            bias[1, e, j] = jnp.where(source > 0.0, scale, 0.0)
-        return carry
-
-    lax.fori_loop(2, EXT - 2, face_step, 0, unroll=2)
-
-    def sweep(n, y_in, y_out):
+            for ref, face in zip(part_.ks, (f_xm, f_xp, f_ym, f_yp, f_zm, f_zp)):
+                ref[e, j] = scale * face
+            source = part_.load(src, e, j)
+            part_.ys[0][0, e, j] = scale * source
+            part_.ys[0][1, e, j] = jnp.where(source > 0.0, scale, 0.0)
+
+    def sweep_step(n, e, part_):
         ratio = COEF[SWEEPS - 2 - n] / LEAD
-
-        def step(e, carry):
-            for j in range(R):
-                ks = [k[e, j] for k in (kxm, kxp, kym, kyp, kzm, kzp)]
-                for f in range(2):
-                    v = y_in[f, e, j]
-                    before = y_in[f, e, j - 1] if j > 0 else pltpu.roll(y_in[f, e, R - 1], 1, 0)
-                    after = y_in[f, e, j + 1] if j < R - 1 else pltpu.roll(y_in[f, e, 0], R - 1, 0)
-                    acc = ratio * bias[f, e, j]
-                    acc = acc + ks[0] * y_in[f, e - 1, j]
-                    acc = acc + ks[1] * y_in[f, e + 1, j]
-                    acc = acc + ks[2] * before
-                    acc = acc + ks[3] * after
-                    acc = acc + ks[4] * z_from_prev(v)
-                    acc = acc + ks[5] * z_from_next(v)
-                    y_out[f, e, j] = acc
+        bias, y_in = part_.ys[0], part_.ys[n]
+        for f in range(2):
+            planes = [y_in[f, e, j] for j in range(part_.count)]
+            befores, afters = part_.around(planes, part_.outer(lambda near, j: near.ys[n][f, e, j]))
+            for j in range(part_.count):
+                ks = [ref[e, j] for ref in part_.ks]
+                acc = ratio * bias[f, e, j]
+                acc = acc + ks[0] * y_in[f, e - 1, j]
+                acc = acc + ks[1] * y_in[f, e + 1, j]
+                acc = acc + ks[2] * befores[j]
+                acc = acc + ks[3] * afters[j]
+                acc = acc + ks[4] * z_from_prev(planes[j])
+                acc = acc + ks[5] * z_from_next(planes[j])
+                if n == SWEEPS - 2:
+                    part_.store(fin.at[f], e, j, acc)
+                else:
+                    part_.ys[n + 1][f, e, j] = acc
+
+    def over_layers(step, low, high, unroll=1):
+        def body(e, carry):
+            step(e)
             return carry
 
-        lax.fori_loop(3 + n, EXT - 3 - n, step, 0, unroll=2)
-
-    bufs = [bias, ya, yb, ya, yb, ya]
-    for n in range(SWEEPS - 1):
-        sweep(n, bufs[n], bufs[n + 1])
-    fin = bufs[SWEEPS - 1]
+        lax.fori_loop(low, high, body, 0, unroll=unroll)
+
+    def set_up_rows(part_):
+        over_layers(lambda e: physical_step(e, part_), 1, EXT - 1, 2)
+
+    def solve_rows(part_):
+        over_layers(lambda e: face_step(e, part_), 2, EXT - 2, 2)
+        for n in range(SWEEPS - 1):
+            over_layers(lambda e, n=n: sweep_step(n, e, part_), 3 + n, EXT - 3 - n, UNROLL[n])
+
+    near = Rows(zh * (YD * R), YD, near_set)
+    beyond = Rows((1 - zh) * (3 * R), YD + 1, far_set, near)
+    wait_tiles(tile_copies[:YD])
+    set_up_rows(near)
+    for k in range(pieces):
+        spread(k)
+    wait_sides(halo_left, halo_right)
+    solve_rows(near)
+    wait_tiles(tile_copies[YD:])
+    set_up_rows(beyond)
+    solve_rows(beyond)
+
+    def row_load(ref, e, k):
+        return jnp.concatenate([ref[e, h, k * R:(k + 1) * R, :] for h in range(halves)], axis=1)
 
     def slab_store(row, value):
         for h in range(halves):
-            part[h, pl.ds(row, R, stride=10 * R), :] = value[:, h * 128:(h + 1) * 128]
+            part[h, pl.ds(row, value.shape[0]), :] = value[:, h * 128:(h + 1) * 128]
 
     def product_step(e, total):
         g = t * R - R + e
         l = e - R
         vm = flag(inside(g - 1))
         vp = flag(inside(g + 1))
-        ps = [fin[0, e, j] for j in range(R)]
-        qs = [fin[1, e, j] for j in range(R)]
-        y_faces = []
-        for j in range(R):
-            pn = around(ps, j)[1]
-            qn = around(qs, j)[1]
-            face = (ps[j] - pn) * (qs[j] - qn)
-            if j == R - 1:
+        ps = [row_load(fin.at[0], e, k) for k in range(R)]
+        qs = [row_load(fin.at[1], e, k) for k in range(R)]
+        down = []
+        for k in range(R):
+            up = min(k + 1, R - 1)
+            pn = jnp.where(y_last, pltpu.roll(ps[up], R - 1, 0), pltpu.roll(ps[k], R - 1, 0))
+            qn = jnp.where(y_last, pltpu.roll(qs[up], R - 1, 0), pltpu.roll(qs[k], R - 1, 0))
+            face = (ps[k] - pn) * (qs[k] - qn)
+            if k == R - 1:
                 face = jnp.where(y_last, 0.0, face)
-            y_faces.append(face)
-        for j in range(R):
-            p, q = ps[j], qs[j]
-            acc = vm * ((p - fin[0, e - 1, j]) * (q - fin[1, e - 1, j]))
-            acc = acc + vp * ((p - fin[0, e + 1, j]) * (q - fin[1, e + 1, j]))
-            acc = acc + y_faces[j] + around(y_faces, j)[0]
+            down.append((face, pltpu.roll(face, 1, 0)))
+        for k in range(R):
+            p, q = ps[k], qs[k]
+            acc = vm * ((p - row_load(fin.at[0], e - 1, k)) * (q - row_load(fin.at[1], e - 1, k)))
+            acc = acc + vp * ((p - row_load(fin.at[0], e + 1, k)) * (q - row_load(fin.at[1], e + 1, k)))
+            above = down[k - 1][1] if k > 0 else 0.0
+            acc = acc + down[k][0] + jnp.where(y_first, above, down[k][1])
             face = jnp.where(z_last, 0.0, (p - z_next(p)) * (q - z_next(q)))
-            acc = (acc + face + z_prev(face)) * wgt[e, j]
-            slab_store(l * R + j, acc)
-            if j == R - 1:
-                edge = jnp.where(y_first, 0.0, pltpu.roll(acc, 1, 0))
-                slab_store(8 * R + l, edge)
-            if j == 0:
-                edge = jnp.where(y_last, 0.0, pltpu.roll(acc, R - 1, 0))
-                slab_store(9 * R + l, edge)
-            total = total + jnp.where(src[e, j] > 0.0, p, 0.0)
+            acc = (acc + face + z_prev(face)) * row_load(wgt, e, k)
+            slab_store(pl.multiple_of(k * 10 * R + l * R, R), acc)
+            if k < R - 1:
+                slab_store((k + 1) * 10 * R + 8 * R + l, acc[R - 1:])
+            if k > 0:
+                slab_store((k - 1) * 10 * R + 9 * R + l, acc[:1])
+            total = total + jnp.where(row_load(src, e, k) > 0.0, p, 0.0)
         return total
 
-    obj_vec = lax.fori_loop(R, 2 * R, product_step, zero, unroll=2)
-
-    def block(case):
-        return pl.ds(pl.multiple_of(case * (10 * R), 10 * R), 10 * R)
-
-    def y_parts(side, dest_base, buf):
+    for h in range(halves):
+        part[h, 8 * R:9 * R, :] = jnp.zeros((R, 128), jnp.float32)
+        part[h, 7 * 10 * R + 9 * R:7 * 10 * R + 10 * R, :] = jnp.zeros((R, 128), jnp.float32)
+
+    obj_vec = lax.fori_loop(R, R + RL, product_step, zero)
+
+    def part_rows(case, a):
+        return pl.ds(pl.multiple_of(case * (10 * R) + a * RL * R, R), RL * R)
+
+    def y_parts(side, dest_base, a, buf):
+        rows = pl.ds(a * RL * R, RL * R)
         return [
             [
                 push(remote(
-                    part.at[h, block(dest_base + (yy + d) % YD)], buf.at[d - 1, h],
-                    s_p.at[side, d - 1, h], r_p.at[side, d - 1, h], {"case": y_case(d), "tile": t},
+                    part.at[h, part_rows(dest_base + (yy + d) % YD, a)], buf.at[d - 1, h, rows],
+                    s_p.at[side, d - 1, h, a], r_p.at[side, d - 1, h, a], {"case": y_case(d), "tile": t},
                 ))
                 for d in range(1, YD)
             ]
             for h in range(halves)
         ]
 
-    def add_parts(h, case, buf, out):
+    def add_parts(h, case, a, buf, out):
         base = case * (10 * R)
 
         def step(i, carry):
@@ -501,49 +554,64 @@
             out[h, rows, :] = (mine + buf[0, h, rows, :]) + (buf[1, h, rows, :] + buf[2, h, rows, :])
             return carry
 
-        lax.fori_loop(0, 10, step, 0, unroll=5)
-
-    far_parts = y_parts(0, far, rfar)
+        lax.fori_loop(a * RL, (a + 1) * RL, step, 0, unroll=RL)
+
+    far_parts = [y_parts(0, far, 0, rfar)]
+    obj_vec = lax.fori_loop(R + RL, 2 * R, product_step, obj_vec)
+    far_parts.append(y_parts(0, far, 1, rfar))
+    near_parts = [y_parts(1, zh * YD, a, rnear) for a in range(2)]
     obj_part = LEAD * jnp.sum(obj_vec, axis=(0, 1), keepdims=True)
+
+    low = pl.ds(0, R)
+    high = pl.ds((R - 1) * R, R)
+    left_case = {"case": far_case, "tile": jnp.maximum(t - 1, 0)}
+    right_case = {"case": far_case, "tile": jnp.minimum(t + 1, tiles - 1)}
+    far_left = remote(fsum.at[:, low], rhalo.at[1], s_q.at[0], r_q.at[1], left_case)
+    far_right = remote(fsum.at[:, high], rhalo.at[0], s_q.at[1], r_q.at[0], right_case)
+    near_left = to_left(nsum.at[:, low], nhalo.at[1], s_q.at[2], r_q.at[3])
+    near_right = to_right(nsum.at[:, high], nhalo.at[0], s_q.at[3], r_q.at[2])
     crossing = []
-    for h in range(halves):
-        for cp in far_parts[h]:
-            cp.wait_recv()
-        add_parts(h, far_case, rfar, fsum)
-        crossing.append(push(remote(fsum.at[h], rz.at[h], s_pz.at[h], r_pz.at[h], z_dev(zl_n))))
-    near_parts = y_parts(1, zh * YD, rnear)
-    for h in range(halves):
-        for cp in near_parts[h]:
-            cp.wait_recv()
-        add_parts(h, c, rnear, qsum)
-    for h in range(halves):
-        crossing[h].wait_recv()
-        qsum[h] = qsum[h] + rz[h]
-
-    q_left = to_left(qsum.at[:, pl.ds(0, R), :], qhalo.at[1], s_q.at[0], r_q.at[1])
-    q_right = to_right(qsum.at[:, pl.ds(7 * R, R), :], qhalo.at[0], s_q.at[1], r_q.at[0])
-    send_sides([q_left], [q_right])
+    for a in range(2):
+        rows = pl.ds(a * RL * R, RL * R)
+        for h in range(halves):
+            for cp in far_parts[a][h]:
+                cp.wait_recv()
+            add_parts(h, far_case, a, rfar, fsum)
+            crossing.append(push(remote(
+                fsum.at[h, rows], rz.at[h, rows], s_pz.at[h, a], r_pz.at[h, a], z_dev(zl_n)
+            )))
+        send_sides([far_left] if a == 0 else [], [] if a == 0 else [far_right])
+    for a in range(2):
+        for h in range(halves):
+            for cp in near_parts[a][h]:
+                cp.wait_recv()
+            add_parts(h, c, a, rnear, nsum)
+    send_sides([near_left], [near_right])
+    for cp in crossing:
+        cp.wait_recv()
 
     @pl.when(has_left)
     def _():
-        q_right.wait_recv()
+        near_right.wait_recv()
+        far_right.wait_recv()
 
     @pl.when(has_right)
     def _():
-        q_left.wait_recv()
-
-    def wide(ref, rows):
-        return jnp.concatenate([ref[h, rows, :] for h in range(halves)], axis=1)
+        near_left.wait_recv()
+        far_left.wait_recv()
+
+    def wide(first, second, rows):
+        return jnp.concatenate([first[h, rows, :] + second[h, rows, :] for h in range(halves)], axis=1)
 
     every = slice(0, R)
-    qs = [wide(qhalo.at[0], every)]
-    qs += [wide(qsum, slice(l * R, (l + 1) * R)) for l in range(R)]
-    qs += [wide(qhalo.at[1], every)]
+    qs = [wide(nhalo.at[0], rhalo.at[0], every)]
+    qs += [wide(nsum, rz, slice(l * R, (l + 1) * R)) for l in range(R)]
+    qs += [wide(nhalo.at[1], rhalo.at[1], every)]
     abs_vec = zero
     for l in range(R):
         v = qs[l + 1]
-        before = jnp.where(y_first, wide(qsum, slice(8 * R + l, 8 * R + l + 1)), pltpu.roll(v, 1, 0))
-        after = jnp.where(y_last, wide(qsum, slice(9 * R + l, 9 * R + l + 1)), pltpu.roll(v, R - 1, 0))
+        before = jnp.where(y_first, wide(nsum, rz, slice(8 * R + l, 8 * R + l + 1)), pltpu.roll(v, 1, 0))
+        after = jnp.where(y_last, wide(nsum, rz, slice(9 * R + l, 9 * R + l + 1)), pltpu.roll(v, R - 1, 0))
         value = (
             2.0 * v + qs[l] + qs[l + 2] + before + after
             + jnp.where(z_first, 0.0, z_prev(v)) + jnp.where(z_last, 0.0, z_next(v))
@@ -558,9 +626,14 @@
         [(arx, s_ax, r_ax, YD * XC, plane_dev), (arz, s_az, r_az, z_n, z_dev)]
     ):
         msg[i] = now
+        before = list(sends)
         copies = [
             push(remote(msg.at[i], buf.at[k - 1], ssem.at[k - 1], rsem.at[k - 1], dev(k))) for k in range(1, count)
         ]
+        if i == 1:
+            sends[:] = before
+            drain()
+            sends[:] = [(None, cp) for cp in copies]
         for cp in copies:
             cp.wait_recv()
         for k in range(1, count):
@@ -578,7 +651,6 @@
 def body(density, heat_power, laser_mask, sink_mask):
     tiles = lax.axis_size("tile")
     rows, grid_y, width = sink_mask.shape
-    planes = (R, R, width)
     halves = width // 128
     pieces = halves * R // HL
     f32 = jnp.float32
@@ -596,16 +668,20 @@
         vm(rows, halves, grid_y, 128),
         pltpu.VMEM((rows, halves, grid_y, 128), jnp.int32),
         pltpu.VMEM((EXT, halves, grid_y, 128), jnp.int32),
-        vm(EXT, *planes),
-        vm(EXT, *planes),
-        vm(EXT, *planes),
-    ] + [vm(EXT, *planes)] * 6 + [vm(2, EXT, *planes)] * 3 + [
+        vm(EXT, halves, grid_y, 128),
+        vm(EXT, halves, grid_y, 128),
+        vm(2, EXT, halves, grid_y, 128),
+    ]
+    for count in (YD, YD + 1):
+        scratch += [vm(EXT, count, R, width)] * 7 + [vm(2, EXT, count, R, width)] * (SWEEPS - 1)
+    scratch += [
         vm(halves, 8 * 10 * R, 128),
         vm(YD - 1, halves, 10 * R, 128),
         vm(YD - 1, halves, 10 * R, 128),
         vm(halves, 10 * R, 128),
         vm(halves, 10 * R, 128),
         vm(halves, 10 * R, 128),
+        vm(2, halves, R, 128),
         vm(2, halves, R, 128),
         vm(R, R, width),
         vm(2, 1, 128),
@@ -620,9 +696,9 @@
         dma(2, YD), dma(2, YD),
         dma(2, YD, pieces), dma(2, YD, pieces),
         dma(4), dma(4),
-        dma(2, YD - 1, halves), dma(2, YD - 1, halves),
-        dma(halves), dma(halves),
-        dma(2), dma(2),
+        dma(2, YD - 1, halves, 2), dma(2, YD - 1, halves, 2),
+        dma(halves, 2), dma(halves, 2),
+        dma(4), dma(4),
         dma(YD * XC - 1), dma(YD * XC - 1),
         dma(z_n - 1), dma(z_n - 1),
     ]

time: 84.3 us -> 80.2 us (0.951)
  Pallas kernels: 80.8 us -> 76.8 us
    pallas_call x1, Pallas kernels: 80.8 us -> 76.8 us  [body(): pl.pallas_call(functools.partial(kernel, tiles), out_shape=(jax.ShapeDtyp...]
where the time goes in v3:
time: 80.2 us; the launch traced here: 80.1 us
  Pallas kernels  76.8 us (96%)
  between operations  1.81 us (2%)
  local copies, waits for them, and re-layouts  1.46 us (2%)
    pallas_call x1, Pallas kernels, body(): pl.pallas_call(functools.partial(kernel, tiles), out_shape=(jax.ShapeDtyp...  76.8 us

profile of v3, /device:TPU:1, one launch (start us, length us, event | category | flops | bytes accessed | tf_op | source)
XLA Modules:
  0.0 80.1 jit_solution(2859448827301183472)
XLA Ops:
  0.6 0.0 copy-start
  0.6 0.8 %copy-done = f32[8,8,256]{2,1,0:T(8,128)S(1)} copy-done((f32[8,8,256]{2,1,0:T(8,128)S(1)}, f32[8,8,256]{2,1,0:T(8,128)}, u32[]{:S(2)}) %copy-start) | copy-done | bytes 65560
  1.5 76.8 %shard_map.59 = (f32[8,8,256]{2,1,0:T(8,128)S(1)}, f32[1,128]{1,0:T(1,128)S(1)}) custom-call(f32[8,8,256]{2,1,0:T(8,128)S(1)} %copy-done, f32[1,8,64,256]{3,2,1,0:T(8,128)} %heat_in.1, s32[1,8,64,256]{3,2,1,0:T(8,128)} %laser_in.1, s32[8,64,256]{2,1,0:T(8,128)} %sink_in.1), custom_call_target="tpu_custom_call" | custom-call | tf_op jit(solution)/shard_map/pallas_call | solution.py:707
  78.3 0.6 copy.8
Async XLA Ops:
  0.6 0.8 %copy-start = (f32[8,8,256]{2,1,0:T(8,128)S(1)}, f32[8,8,256]{2,1,0:T(8,128)}, u32[]{:S(2)}) copy-start(f32[8,8,256]{2,1,0:T(8,128)} %dens_in.1) | copy-start | bytes 196612

commit v4 on v3

--- a/solution.py
+++ b/solution.py
@@ -189,8 +189,11 @@
     via = []
     for k in range(pieces):
         way = quarter if k < pieces // 2 else z_n - quarter
-        way = jnp.where(column == 0, quarter, way)
-        via.append(jnp.where(column == XC // 2 - 1, z_n - quarter, way))
+        if k < pieces - 1:
+            way = jnp.where(column == 0, quarter, way)
+        if k > 0:
+            way = jnp.where(column == XC // 2 - 1, z_n - quarter, way)
+        via.append(way)
     for k in range(pieces):
         push(remote(piece_in(k), relay.at[k], s_zr.at[k], r_zr.at[k], z_dev(via[k])))
     y_copies = []
@@ -464,11 +467,13 @@
 
         lax.fori_loop(low, high, body, 0, unroll=unroll)
 
-    def set_up_rows(part_):
-        over_layers(lambda e: physical_step(e, part_), 1, EXT - 1, 2)
+    def set_up_rows(part_, low=1, high=EXT - 1):
+        over_layers(lambda e: physical_step(e, part_), low, high, 2)
+
+    def face_rows(part_, low=2, high=EXT - 2):
+        over_layers(lambda e: face_step(e, part_), low, high, 2)
 
     def solve_rows(part_):
-        over_layers(lambda e: face_step(e, part_), 2, EXT - 2, 2)
         for n in range(SWEEPS - 1):
             over_layers(lambda e, n=n: sweep_step(n, e, part_), 3 + n, EXT - 3 - n, UNROLL[n])
 
@@ -479,9 +484,15 @@
     for k in range(pieces):
         spread(k)
     wait_sides(halo_left, halo_right)
+    face_rows(near)
     solve_rows(near)
+    set_up_rows(beyond, R + 1, 2 * R - 1)
+    face_rows(beyond, R + 2, 2 * R - 2)
     wait_tiles(tile_copies[YD:])
-    set_up_rows(beyond)
+    set_up_rows(beyond, 1, R + 1)
+    set_up_rows(beyond, 2 * R - 1, EXT - 1)
+    face_rows(beyond, 2, R + 2)
+    face_rows(beyond, 2 * R - 2, EXT - 2)
     solve_rows(beyond)
 
     def row_load(ref, e, k):
@@ -622,13 +633,18 @@
     pl.semaphore_wait(round_sem.at[1], len(met))
     lane1 = lax.broadcasted_iota(jnp.int32, (1, 128), 1)
     now = jnp.where(lane1 == 8, jnp.sum(abs_vec, axis=(0, 1), keepdims=True), jnp.where(lane1 == c, obj_part, 0.0))
-    for i, (buf, ssem, rsem, count, dev) in enumerate(
-        [(arx, s_ax, r_ax, YD * XC, plane_dev), (arz, s_az, r_az, z_n, z_dev)]
+    def ring(d, n):
+        return min(d, n - d)
+
+    plane_order = sorted(range(1, YD * XC), key=lambda k: -ring(k // XC, YD) - ring(k % XC, XC) / 2)
+    z_order = sorted(range(1, z_n), key=lambda k: -ring(k, z_n))
+    for i, (buf, ssem, rsem, order, dev) in enumerate(
+        [(arx, s_ax, r_ax, plane_order, plane_dev), (arz, s_az, r_az, z_order, z_dev)]
     ):
         msg[i] = now
         before = list(sends)
         copies = [
-            push(remote(msg.at[i], buf.at[k - 1], ssem.at[k - 1], rsem.at[k - 1], dev(k))) for k in range(1, count)
+            push(remote(msg.at[i], buf.at[k - 1], ssem.at[k - 1], rsem.at[k - 1], dev(k))) for k in order
         ]
         if i == 1:
             sends[:] = before
@@ -636,8 +652,7 @@
             sends[:] = [(None, cp) for cp in copies]
         for cp in copies:
             cp.wait_recv()
-        for k in range(1, count):
-            now = now + buf[k - 1]
+        now = now + jnp.sum(buf[...], axis=0)
 
     total_abs = jnp.sum(jnp.where(lane1 == 8, now, 0.0), axis=(0, 1), keepdims=True)
     scale = 1.0 / (total_abs / (grid_rows * R * R * width) + 1e-06)

time: 80.2 us -> 78.6 us (0.980)
  Pallas kernels: 76.8 us -> 75.1 us
    pallas_call x1, Pallas kernels: 76.8 us -> 75.1 us  [body(): pl.pallas_call(functools.partial(kernel, tiles), out_shape=(jax.ShapeDtyp...]
where the time goes in v4:
time: 78.6 us; the launch traced here: 78.4 us
  Pallas kernels  75.1 us (96%)
  between operations  1.81 us (2%)
  local copies, waits for them, and re-layouts  1.46 us (2%)
    pallas_call x1, Pallas kernels, body(): pl.pallas_call(functools.partial(kernel, tiles), out_shape=(jax.ShapeDtyp...  75.1 us

profile of v4, /device:TPU:1, one launch (start us, length us, event | category | flops | bytes accessed | tf_op | source)
XLA Modules:
  0.0 78.4 jit_solution(17607459442607867913)
XLA Ops:
  0.6 0.0 copy-start
  0.6 0.8 %copy-done = f32[8,8,256]{2,1,0:T(8,128)S(1)} copy-done((f32[8,8,256]{2,1,0:T(8,128)S(1)}, f32[8,8,256]{2,1,0:T(8,128)}, u32[]{:S(2)}) %copy-start) | copy-done | bytes 65560
  1.5 75.1 %shard_map.59 = (f32[8,8,256]{2,1,0:T(8,128)S(1)}, f32[1,128]{1,0:T(1,128)S(1)}) custom-call(f32[8,8,256]{2,1,0:T(8,128)S(1)} %copy-done, f32[1,8,64,256]{3,2,1,0:T(8,128)} %heat_in.1, s32[1,8,64,256]{3,2,1,0:T(8,128)} %laser_in.1, s32[8,64,256]{2,1,0:T(8,128)} %sink_in.1), custom_call_target="tpu_custom_call" | custom-call | tf_op jit(solution)/shard_map/pallas_call | solution.py:722
  76.6 0.6 copy.8
Async XLA Ops:
  0.6 0.8 %copy-start = (f32[8,8,256]{2,1,0:T(8,128)S(1)}, f32[8,8,256]{2,1,0:T(8,128)}, u32[]{:S(2)}) copy-start(f32[8,8,256]{2,1,0:T(8,128)} %dens_in.1) | copy-start | bytes 196612

commit v5 on v4

--- a/solution.py
+++ b/solution.py
@@ -481,10 +481,10 @@
     beyond = Rows((1 - zh) * (3 * R), YD + 1, far_set, near)
     wait_tiles(tile_copies[:YD])
     set_up_rows(near)
+    wait_sides(halo_left, halo_right)
+    face_rows(near)
     for k in range(pieces):
         spread(k)
-    wait_sides(halo_left, halo_right)
-    face_rows(near)
     solve_rows(near)
     set_up_rows(beyond, R + 1, 2 * R - 1)
     face_rows(beyond, R + 2, 2 * R - 2)
@@ -729,7 +729,7 @@
         out_specs=(vmem_spec, vmem_spec),
         scratch_shapes=scratch,
         compiler_params=pltpu.CompilerParams(
-            collective_id=0, has_side_effects=True, vmem_limit_bytes=56150000
+            collective_id=0, has_side_effects=True, vmem_limit_bytes=56460000
         ),
     )(density, heat_power, laser_mask, sink_mask)
     return sensitivity, objective[0, :1]

time: 78.6 us -> 77.6 us (0.987)
  local copies, waits for them, and re-layouts: 1.46 us -> 0.63 us
    unnamed x3 -> x1, local copies, waits for them, and re-layouts: 1.46 us -> 0.63 us
where the time goes in v5:
time: 77.6 us; the launch traced here: 77.5 us
  Pallas kernels  75.1 us (97%)
  between operations  1.8 us (2%)
    pallas_call x1, Pallas kernels, body(): pl.pallas_call(functools.partial(kernel, tiles), out_shape=(jax.ShapeDtyp...  75.1 us

profile of v5, /device:TPU:1, one launch (start us, length us, event | category | flops | bytes accessed | tf_op | source)
XLA Modules:
  0.0 77.5 jit_solution(17213807268190126374)
XLA Ops:
  0.6 75.1 %shard_map.59 = (f32[8,8,256]{2,1,0:T(8,128)S(1)}, f32[1,128]{1,0:T(1,128)S(1)}) custom-call(f32[8,8,256]{2,1,0:T(8,128)} %dens_in.1, f32[1,8,64,256]{3,2,1,0:T(8,128)} %heat_in.1, s32[1,8,64,256]{3,2,1,0:T(8,128)} %laser_in.1, s32[8,64,256]{2,1,0:T(8,128)} %sink_in.1), custom_call_target="tpu_custom_call" | custom-call | tf_op jit(solution)/shard_map/pallas_call | solution.py:722
  75.7 0.6 copy.8

commit v6 on v5

--- a/solution.py
+++ b/solution.py
@@ -237,6 +237,7 @@
         for h in range(halves):
             loads[h][k].wait()
     lax.fori_loop(0, R, make_source, 0)
+    send_sides(halo_left[:1], halo_right[:1])
 
     def slab_of(case):
         return pl.ds(pl.multiple_of(case * R, R), R)
@@ -265,7 +266,6 @@
             cp.wait_recv()
         forward(zh * YD + (yy + YD - d) % YD, d)
 
-    send_sides(halo_left[:1], halo_right[:1])
 
     z_copies = []
     for k in range(pieces):

time: 77.6 us -> 77.1 us (level)
  no operation moved by 1% of the time
where the time goes in v6:
time: 77.1 us; the launch traced here: 76.9 us
  Pallas kernels  74.5 us (97%)
  between operations  1.8 us (2%)
    pallas_call x1, Pallas kernels, body(): pl.pallas_call(functools.partial(kernel, tiles), out_shape=(jax.ShapeDtyp...  74.5 us

profile of v6, /device:TPU:1, one launch (start us, length us, event | category | flops | bytes accessed | tf_op | source)
XLA Modules:
  0.0 76.9 jit_solution(15169637609707143980)
XLA Ops:
  0.6 74.5 %shard_map.59 = (f32[8,8,256]{2,1,0:T(8,128)S(1)}, f32[1,128]{1,0:T(1,128)S(1)}) custom-call(f32[8,8,256]{2,1,0:T(8,128)} %dens_in.1, f32[1,8,64,256]{3,2,1,0:T(8,128)} %heat_in.1, s32[1,8,64,256]{3,2,1,0:T(8,128)} %laser_in.1, s32[8,64,256]{2,1,0:T(8,128)} %sink_in.1), custom_call_target="tpu_custom_call" | custom-call | tf_op jit(solution)/shard_map/pallas_call | solution.py:722
  75.1 0.6 copy.8
